TPU v7x, 32 devices: a whole 2x2x4 slice. The times are simulated.
32 devices in a mesh: wide: 16 (over z, y, x), narrow: 2 (over core).
Axes of the slice: x: 2, y: 2, z: 4, core: 2. Of those that a mesh axis runs over, the one named last changes fastest.
Arguments:
- data: float32 [16384, 512], P(('wide', 'narrow')), may hold values from -200 to 200, as said below
- anchors: int32 [64], replicated, may hold values from 0 to 511, as said below
Outputs:
- factor: float32 [512, 512], replicated
- coeffs: float32 [64, 512], replicated
- basis: float32 [16384, 512], P(('wide', 'narrow'))
- resid_norms: float32 [512], replicated
Inputs may be any that keep to these rules, and one draw needn't show every extreme that they name: `data`: the entries are finite real numbers. `anchors`: 64 distinct column numbers.
All inputs are finite; a program needn't handle non-finite values.
Results may differ from a plain program's by a relative error of at most 0.0003.
Values sent between devices are 32-bit elements; how exact they have to be, the bound alone decides.
No kernel may reach another device: no remote copies, remote signals or barrier semaphores. Data moves between devices by JAX's collectives and lax.ppermute only.
A program may use at most 64 MiB of HBM per device.

v0:
```python
import functools

import jax
import jax.numpy as jnp
from jax import lax
from jax.experimental import pallas as pl
from jax.experimental.pallas import tpu as pltpu
from jax.sharding import PartitionSpec as P

AXES = ("wide", "narrow")
NN = (((1,), (0,)), ((), ()))
NT = (((1,), (1,)), ((), ()))
TN = (((0,), (0,)), ((), ()))
PANEL = 32
LEFT = (0, 0, 1, 0, 2, 1)
RIGHT = (0, 1, 0, 2, 0, 1)


def thirds(x):
    hi = x.astype(jnp.bfloat16)
    rest = x - hi.astype(jnp.float32)
    mid = rest.astype(jnp.bfloat16)
    low = (rest - mid.astype(jnp.float32)).astype(jnp.bfloat16)
    return (hi, mid, low)


def bdot(a, b, dims):
    return lax.dot_general(a, b, dims, preferred_element_type=jnp.float32)


def six(a, b, dims):
    ca, cb = dims[0][0][0], dims[0][1][0]
    left = jnp.concatenate([a[i] for i in LEFT], axis=ca)
    right = jnp.concatenate([b[i] for i in RIGHT], axis=cb)
    return bdot(left, right, dims)


def mm(a, b, dims=NN):
    return six(thirds(a), thirds(b), dims)


def mm_pick(a, pick, dims):
    return sum(bdot(t, pick, dims) for t in thirds(a))


def rsq(p):
    r = lax.rsqrt(p)
    return r * (1.5 - (0.5 * p) * (r * r))


def lane(x, c):
    return jnp.broadcast_to(x[:, c : c + 1], (8, 128))


def sub(x, i):
    return jnp.take_along_axis(x, jnp.full((8, 128), i, jnp.int32), axis=0, mode="promise_in_bounds")


def eliminate(rows, c0, s_ref):
    a = rows[0][0]
    for k in range(8):
        s_ref[8 * k : 8 * k + 8, :] = lane(a, c0 + k)
    d = {
        (i, k): jnp.broadcast_to(s_ref[8 * k + i : 8 * k + i + 1, :], (8, 128)) for i in range(8) for k in range(i + 1)
    }
    n = [lax.rsqrt(d[i, i]) for i in range(8)]
    d = {(i, k): (v * n[i]) * n[k] for (i, k), v in d.items()}
    ru = [[sub(x, i) * n[i] for x in rows[0]] for i in range(8)]
    cols = [[lane(t[0], c0 + k) * n[k] for k in range(8)] for t in rows[1:]]
    later = [list(t) for t in rows[1:]]
    row = lax.broadcasted_iota(jnp.int32, (8, 128), 0)
    out = [jnp.zeros((8, 128), jnp.float32) for _ in rows[0]]
    low = {}
    for b in (0, 4):
        below = range(b, 8)
        e = {}
        for i in below:
            e[i, 0] = d[i, b]
        p = [d[b, b]]
        for j in range(1, 4):
            for i in range(b + j, 8):
                v = p[0] * d[i, b + j] - e[i, 0] * e[b + j, 0]
                for m in range(1, j):
                    v = p[m] * v - e[i, m] * e[b + j, m]
                e[i, j] = v
            p.append(e[b + j, j])
        rho = [rsq(x) for x in p]
        root = [x * r for x, r in zip(p, rho)]
        inv = [rho[0]]
        acc = root[0]
        for j in range(1, 4):
            inv.append(rho[j] * acc)
            acc = acc * root[j]
        sig = rho[0]
        for j in range(4):
            if j:
                sig = sig * rho[j]
            for i in range(b + j + 1, 8):
                low[i, b + j] = e[i, j] * sig
        if b == 0:
            for i in range(4, 8):
                for k in range(4, i + 1):
                    x = low[i, 0] * low[k, 0] + low[i, 1] * low[k, 1]
                    y = low[i, 2] * low[k, 2] + low[i, 3] * low[k, 3]
                    d[i, k] = d[i, k] - (x + y)
        for j in range(4):
            r, at = inv[j], b + j
            u = [x * r for x in ru[at]]
            for i in range(at + 1, 8):
                ru[i] = [x - low[i, at] * y for x, y in zip(ru[i], u)]
            out = [jnp.where(row == at, y, x) for x, y in zip(out, u)]
            for t, c in enumerate(cols):
                f = c[at] * r
                for k in range(at + 1, 8):
                    c[k] = c[k] - f * low[k, at]
                later[t] = [x - f * y for x, y in zip(later[t], u)]
    return out, later


def tri_upper(x):
    r = lax.broadcasted_iota(jnp.int32, x.shape, 0)
    c = lax.broadcasted_iota(jnp.int32, x.shape, 1)
    return jnp.where(r <= c, x, 0.0)


def eye(n, m):
    r = lax.broadcasted_iota(jnp.int32, (n, m), 0)
    c = lax.broadcasted_iota(jnp.int32, (n, m), 1)
    return (r == c).astype(jnp.float32)


def cholesky_steps(t_ref, e_ref, s_ref, size, blocks, done):
    later = []
    for k in range(blocks):
        r0, c0 = k * size, k * 128
        e_ref[r0 : r0 + size, :] = eye(size, 128)
        for p in range(size // PANEL):
            base = r0 + p * PANEL
            width = blocks - k
            tiles = []
            for t in range(PANEL // 8):
                at = slice(base + 8 * t, base + 8 * t + 8)
                tiles.append(
                    [t_ref[at, c0 + 128 * w : c0 + 128 * w + 128] for w in range(width)] + [e_ref[at, :]]
                )
            outs = []
            steps = PANEL // 8
            for t in range(steps):
                out, tiles = eliminate(tiles, p * PANEL + 8 * t, s_ref.at[(p * steps + t) % 8])
                outs.append(out)
                for _ in range(-(-len(later) // (steps - t))):
                    later.pop(0)()
                yield
            full = [jnp.concatenate([o[w] for o in outs], axis=0) for w in range(width + 1)]
            for w in range(width):
                t_ref[base : base + PANEL, c0 + 128 * w : c0 + 128 * w + 128] = full[w]
            e_ref[base : base + PANEL, :] = full[width]
            split = [thirds(x) for x in full]
            left = [jnp.concatenate([s[i] for i in LEFT], axis=0) for s in split]
            right = [jnp.concatenate([s[i] for i in RIGHT], axis=0) for s in split]
            last = base + PANEL == r0 + size

            def update(w, lo, hi, flip, r0=r0, c0=c0, width=width, right=right):
                both = bdot(flip[lo:hi], jnp.concatenate(right[w:] if w == 0 else right[w:width], axis=1), NN)
                rows = slice(r0 + size * w + lo, r0 + size * w + hi)
                at = slice(c0 + 128 * w, c0 + 128 * width)
                t_ref[rows, at] = t_ref[rows, at] - both[:, : 128 * (width - w)]
                if w == 0:
                    e_ref[rows, :] = e_ref[rows, :] - both[:, 128 * width :]

            for w in range(1 if last else 0, width):
                lo = 0 if w else (p + 1) * PANEL
                flip = left[w].T
                first = w == (1 if last else 0)
                if first:
                    update(w, lo, lo + PANEL, flip)
                    lo += PANEL
                if lo < size:
                    later.append(functools.partial(update, w, lo, size, flip))
            if last:
                done(k)


def main_kernel(total, pieces, data_ref, anc_ref, fac_out, coef_out, bas_out, res_out, t_ref, e_ref, y_ref, f_ref, td_ref, ed_ref, rk_ref, cf_ref, sq_ref, s_ref, g_ref, sem):
    nb = 4
    n_rows = data_ref.shape[0]
    copies = []
    queue = []
    state = {}

    def send(src, dst, n):
        c = pltpu.make_async_copy(src, dst, sem.at[n])
        c.start()
        copies.append(c)

    place_pieces(pieces, t_ref, g_ref, total)
    lanes = lax.broadcasted_iota(jnp.int32, (64, 512), 1)
    pick = (anc_ref[...] == lanes).astype(jnp.bfloat16)

    def side_steps():
        sums = [None] * nb
        for i in range(nb):
            for j in range(i, nb):
                g = thirds(state["gram"][i, j])
                pi, pj = pick[:, 128 * i : 128 * i + 128], pick[:, 128 * j : 128 * j + 128]
                for x in g:
                    v = bdot(pi, x, NN)
                    sums[j] = v if sums[j] is None else sums[j] + v
                    if i < j:
                        v = bdot(pj, x, NT)
                        sums[i] = v if sums[i] is None else sums[i] + v
                if j % 2:
                    yield
        rows_k = jnp.concatenate(sums, axis=1)
        rk_ref[...] = rows_k
        wide = jnp.concatenate([pick, jnp.zeros((64, 512), jnp.bfloat16)], axis=0)
        td_ref[...] = mm_pick(rows_k, wide, NT)
        yield
        yield from cholesky_steps(td_ref, ed_ref, s_ref.at[1], 64, 1, lambda _: None)
        linv = thirds(ed_ref[:, 0:64])
        z = six(linv, thirds(rk_ref[...]), NN)
        yield
        cf_ref[...] = six(linv, thirds(z), TN)
        send(cf_ref, coef_out, 0)
        state["coef"] = True

    state["gram"] = {
        (i, j): t_ref[128 * i : 128 * i + 128, 128 * j : 128 * j + 128] for i in range(nb) for j in range(i, nb)
    }

    def clear(k):
        if k:
            f_ref[128 * k : 128 * k + 128, 0 : 128 * k] = jnp.zeros((128, 128 * k), jnp.float32)

    for k in range(nb):
        queue.append(functools.partial(clear, k))

    def finished(k):
        lo, hi = 128 * k, 128 * k + 128
        last = k == nb - 1
        src = data_ref if k == 0 else y_ref
        linv = thirds(e_ref[lo:hi, :])
        f_ref[lo:hi, lo:hi] = tri_upper(t_ref[lo:hi, lo:hi])
        if not last:
            f_ref[lo:hi, hi:] = t_ref[lo:hi, hi:]
            above = thirds(t_ref[lo:hi, hi:])

        def rows(n):
            at = slice(128 * n, min(128 * n + 128, n_rows))
            b = six(thirds(src[at, lo:hi]), linv, NT)
            y_ref[at, lo:hi] = b
            if not last:
                y_ref[at, hi:] = src[at, hi:] - six(thirds(b), above, NN)

        for n in range(-(-n_rows // 128)):
            queue.append(functools.partial(rows, n))
        queue.append(functools.partial(residual, k))

        def ship():
            send(f_ref.at[lo:hi, :], fac_out.at[lo:hi, :], 1 + k)
            send(y_ref.at[:, lo:hi], bas_out.at[:, lo:hi], 5 + k)

        queue.append(ship)

    def residual(k):
        lo, hi = 128 * k, 128 * k + 128
        fk = mm_pick(f_ref[lo:hi, lo:], pick[:, lo:], NT)
        diff = f_ref[lo:hi, :] - six(thirds(fk), thirds(cf_ref[...]), NN)
        v = jnp.sum(diff * diff, axis=0, keepdims=True)
        state["sq"] = v if "sq" not in state else state["sq"] + v

    main = cholesky_steps(t_ref, e_ref, s_ref.at[0], 128, nb, finished)
    side = side_steps()
    running = [main, side]
    while running:
        for s in list(running):
            try:
                next(s)
            except StopIteration:
                running.remove(s)
        if queue:
            queue.pop(0)()
    for f in queue:
        f()
    sq_ref[...] = jnp.sqrt(1.0 + state["sq"])
    send(sq_ref, res_out, 9)
    for c in copies:
        c.wait()


def place_pieces(pieces, t_ref, g_ref, total):
    me = my_index()
    core, q = lax.rem(me, 2), lax.rem(me // 2, 4)
    for m in range(8):
        at = (core ^ (m // 4)) * 640 + (q ^ (m % 4)) * 160
        g_ref[pl.ds(pl.multiple_of(at, 160), 160), :] = pieces[m][...]
    n = 0
    for i in range(4):
        for j in range(i, 4):
            x = g_ref[128 * n : 128 * n + 128, :] / total
            t_ref[128 * i : 128 * i + 128, 128 * j : 128 * j + 128] = x
            n += 1


def fit_call(pieces, data, anchors, total):
    f32 = jnp.float32
    count = len(pieces)
    rows = data.shape[0]

    def body(*refs):
        main_kernel(total, refs[:count], *refs[count:])

    vmem = pl.BlockSpec(memory_space=pltpu.VMEM)
    hbm = pl.BlockSpec(memory_space=pl.ANY)
    return pl.pallas_call(
        body,
        out_shape=(
            jax.ShapeDtypeStruct((512, 512), f32),
            jax.ShapeDtypeStruct((64, 512), f32),
            jax.ShapeDtypeStruct((rows, 512), f32),
            jax.ShapeDtypeStruct((1, 512), f32),
        ),
        in_specs=[vmem] * (count + 2),
        out_specs=(hbm,) * 4,
        scratch_shapes=[
            pltpu.VMEM((512, 512), f32),
            pltpu.VMEM((512, 128), f32),
            pltpu.VMEM((rows, 512), f32),
            pltpu.VMEM((512, 512), f32),
            pltpu.VMEM((64, 128), f32),
            pltpu.VMEM((64, 128), f32),
            pltpu.VMEM((64, 512), f32),
            pltpu.VMEM((64, 512), f32),
            pltpu.VMEM((1, 512), f32),
            pltpu.VMEM((2, 8, 64, 128), f32),
            pltpu.VMEM((1280, 128), f32),
            pltpu.SemaphoreType.DMA((10,)),
        ],
        compiler_params=pltpu.CompilerParams(vmem_limit_bytes=32 << 20),
        name="factor_fit",
    )(*pieces, data, anchors.reshape(64, 1))


def my_index():
    return lax.axis_index("wide") * lax.axis_size("narrow") + lax.axis_index("narrow")


def gram_kernel(x_hbm, own_ref, other_ref, x_ref, both_ref, sem):
    rows = x_ref.shape[0] // 4
    copies = []
    for c in range(4):
        at = pl.ds(rows * c, rows)
        copies.append(pltpu.make_async_copy(x_hbm.at[at, :], x_ref.at[at, :], sem.at[c]))
        copies[-1].start()
    for c in range(4):
        copies[c].wait()
        split = thirds(x_ref[rows * c : rows * c + rows, :])
        left = jnp.concatenate([split[i] for i in LEFT], axis=0)
        right = jnp.concatenate([split[i] for i in RIGHT], axis=0)
        n = 0
        for i in range(4):
            row = bdot(left[:, 128 * i : 128 * i + 128], right[:, 128 * i :], TN)
            for j in range(4 - i):
                at = slice(128 * (n % 5), 128 * (n % 5) + 128)
                x = row[:, 128 * j : 128 * j + 128]
                both_ref[n // 5, at, :] = x if c == 0 else both_ref[n // 5, at, :] + x
                n += 1
    bit = lax.rem(my_index(), 2)
    own_ref[...] = both_ref[bit]
    other_ref[...] = both_ref[1 - bit]


def gram_call(x):
    half = jax.ShapeDtypeStruct((640, 128), jnp.float32)
    return pl.pallas_call(
        gram_kernel,
        out_shape=(half, half, jax.ShapeDtypeStruct(x.shape, x.dtype)),
        in_specs=[pl.BlockSpec(memory_space=pltpu.HBM)],
        out_specs=(pl.BlockSpec(memory_space=pltpu.VMEM),) * 3,
        scratch_shapes=[pltpu.VMEM((2, 640, 128), jnp.float32), pltpu.SemaphoreType.DMA((4,))],
        compiler_params=pltpu.CompilerParams(vmem_limit_bytes=16 << 20),
        name="gram",
    )(x)


def split_kernel(own_ref, got_ref, *outs):
    q = lax.rem(my_index() // 2, 4)
    for m, out in enumerate(outs):
        rows = pl.ds(pl.multiple_of((q ^ m) * 160, 160), 160)
        out[...] = own_ref[rows, :] + got_ref[rows, :]


def split_call(own, got):
    part = jax.ShapeDtypeStruct((160, 128), jnp.float32)
    return pl.pallas_call(
        split_kernel,
        out_shape=(part,) * 4,
        compiler_params=pltpu.CompilerParams(vmem_limit_bytes=8 << 20),
        name="split",
    )(own, got)


def swap(x, bit, devices):
    return lax.ppermute(x, AXES, [(i, i ^ bit) for i in range(devices)])


def total_gram(x, devices):
    own, other, kept = gram_call(x)
    parts = split_call(own, swap(other, 1, devices))
    got = [swap(parts[m], 2 * m, devices) for m in (1, 2, 3)]
    piece = (parts[0] + got[0]) + (got[1] + got[2])
    bit = 8
    while bit < devices:
        if bit * 2 < devices:
            far = [swap(piece, bit * m, devices) for m in (1, 2, 3)]
            piece = (piece + far[0]) + (far[1] + far[2])
        else:
            piece = piece + swap(piece, bit, devices)
        bit *= 4
    mine = [piece] + [swap(piece, 2 * m, devices) for m in (1, 2, 3)]
    theirs = [swap(p, 1, devices) for p in mine]
    return mine + theirs, kept


def on_device(data, anchors):
    devices = lax.axis_size("wide") * lax.axis_size("narrow")
    pieces, kept = total_gram(data, devices)
    factor, coeffs, basis, resid = fit_call(pieces, kept, anchors, data.shape[0] * devices)
    return (factor, coeffs, basis, resid.reshape(-1))


def solution(mesh):
    placed = (P(AXES, None), P())
    return jax.shard_map(
        on_device,
        mesh=mesh,
        in_specs=placed,
        out_specs=(P(), P(), P(AXES, None), P()),
        check_vma=False,
    )
```

profile of v0, /device:TPU:0, one launch (start us, length us, event | category | flops | bytes accessed | tf_op | source)
XLA Modules:
  0.0 52.1 jit_solution(5642410828459690418)
XLA Ops:
  0.6 0.0 copy-start
  0.6 1.2 %copy-done = f32[512,512]{1,0:T(8,128)S(1)} copy-done((f32[512,512]{1,0:T(8,128)S(1)}, f32[512,512]{1,0:T(8,128)}, u32[]{:S(2)}) %copy-start) | copy-done | bytes 1048600
  1.9 2.2 %gram.1 = (f32[640,128]{1,0:T(8,128)S(1)}, f32[640,128]{1,0:T(8,128)S(1)}, f32[512,512]{1,0:T(8,128)S(1)}) custom-call(f32[512,512]{1,0:T(8,128)S(1)} %copy-done), custom_call_target="tpu_custom_call" | custom-call | tf_op jit(solution)/shard_map/gram/pallas_call | solution.py:375
  4.1 0.5 collective-permute-start
  4.6 1.3 %collective-permute-done.got_ref = f32[640,128]{1,0:T(8,128)S(1)} collective-permute-done((f32[640,128]{1,0:T(8,128)S(1)}, f32[640,128]{1,0:T(8,128)S(1)}, u32[]{:S(2)}, u32[]{:S(2)}) %collective-permute-start) | collective-permute-done | bytes 327712 | tf_op jit(solution)/shard_map/ppermute | solution.py:404
  5.9 2.9 %collective-permute-start.1 = (f32[160,128]{1,0:T(8,128)S(1)}, f32[160,128]{1,0:T(8,128)S(1)}, u32[]{:S(2)}, u32[]{:S(2)}) collective-permute-start(f32[160,128]{1,0:T(8,128)S(1)} %get-tuple-element.18), channel_id=1, source_target_pairs={{0,2},{1,3},{2,0},{3,1},{4,6},{5,7},{6,4},{7,5},{8,10},{9,11},{10,... | collective-permute-start | bytes 245768 | tf_op jit(solution)/shard_map/ppermute | solution.py:404
  8.8 1.5 %collective-permute-start.2 = (f32[160,128]{1,0:T(8,128)S(1)}, f32[160,128]{1,0:T(8,128)S(1)}, u32[]{:S(2)}, u32[]{:S(2)}) collective-permute-start(f32[160,128]{1,0:T(8,128)S(1)} %get-tuple-element.19), channel_id=1, source_target_pairs={{0,4},{1,5},{2,6},{3,7},{4,0},{5,1},{6,2},{7,3},{8,12},{9,13},{10,... | collective-permute-start | bytes 245768 | tf_op jit(solution)/shard_map/ppermute | solution.py:404
  10.4 0.0 collective-permute-start.3
  10.4 1.2 %collective-permute-done.1 = f32[160,128]{1,0:T(8,128)S(1)} collective-permute-done((f32[160,128]{1,0:T(8,128)S(1)}, f32[160,128]{1,0:T(8,128)S(1)}, u32[]{:S(2)}, u32[]{:S(2)}) %collective-permute-start.1) | collective-permute-done | bytes 81952 | tf_op jit(solution)/shard_map/ppermute | solution.py:404
  11.6 2.5 %collective-permute-done.2 = f32[160,128]{1,0:T(8,128)S(1)} collective-permute-done((f32[160,128]{1,0:T(8,128)S(1)}, f32[160,128]{1,0:T(8,128)S(1)}, u32[]{:S(2)}, u32[]{:S(2)}) %collective-permute-start.2) | collective-permute-done | bytes 81952 | tf_op jit(solution)/shard_map/ppermute | solution.py:404
  14.1 1.6 %collective-permute-done.3 = f32[160,128]{1,0:T(8,128)S(1)} collective-permute-done((f32[160,128]{1,0:T(8,128)S(1)}, f32[160,128]{1,0:T(8,128)S(1)}, u32[]{:S(2)}, u32[]{:S(2)}) %collective-permute-start.3) | collective-permute-done | bytes 81952 | tf_op jit(solution)/shard_map/ppermute | solution.py:404
  15.7 3.7 %collective-permute-start.6 = (f32[160,128]{1,0:T(8,128)S(1)}, f32[160,128]{1,0:T(8,128)S(1)}, u32[]{:S(2)}, u32[]{:S(2)}) collective-permute-start(f32[160,128]{1,0:T(8,128)S(1)} %add_add_fusion.1), channel_id=1, source_target_pairs={{0,24},{1,25},{2,26},{3,27},{4,28},{5,29},{6,30},{7,31},{8,16},{9,... | collective-permute-start | bytes 245768 | tf_op jit(solution)/shard_map/ppermute | solution.py:404
  19.4 0.0 collective-permute-start.5
  19.4 0.8 %collective-permute-start.4 = (f32[160,128]{1,0:T(8,128)S(1)}, f32[160,128]{1,0:T(8,128)S(1)}, u32[]{:S(2)}, u32[]{:S(2)}) collective-permute-start(f32[160,128]{1,0:T(8,128)S(1)} %add_add_fusion.1), channel_id=1, source_target_pairs={{0,8},{1,9},{2,10},{3,11},{4,12},{5,13},{6,14},{7,15},{8,0},{9,1},... | collective-permute-start | bytes 245768 | tf_op jit(solution)/shard_map/ppermute | solution.py:404
  20.2 1.9 %collective-permute-done.6 = f32[160,128]{1,0:T(8,128)S(1)} collective-permute-done((f32[160,128]{1,0:T(8,128)S(1)}, f32[160,128]{1,0:T(8,128)S(1)}, u32[]{:S(2)}, u32[]{:S(2)}) %collective-permute-start.6) | collective-permute-done | bytes 81952 | tf_op jit(solution)/shard_map/ppermute | solution.py:404
  22.0 3.3 %collective-permute-done.5 = f32[160,128]{1,0:T(8,128)S(1)} collective-permute-done((f32[160,128]{1,0:T(8,128)S(1)}, f32[160,128]{1,0:T(8,128)S(1)}, u32[]{:S(2)}, u32[]{:S(2)}) %collective-permute-start.5) | collective-permute-done | bytes 81952 | tf_op jit(solution)/shard_map/ppermute | solution.py:404
  25.3 0.0 collective-permute-done.4
  25.3 0.0 copy-start.1
  25.3 0.9 %collective-permute-start.9 = (f32[160,128]{1,0:T(8,128)S(1)}, f32[160,128]{1,0:T(8,128)S(1)}, u32[]{:S(2)}, u32[]{:S(2)}) collective-permute-start(f32[160,128]{1,0:T(8,128)S(1)} %add_add_fusion.refs_0_), channel_id=1, source_target_pairs={{0,6},{1,7},{2,4},{3,5},{4,2},{5,3},{6,0},{7,1},{8,14},{9,15},{10,... | collective-permute-start | bytes 245768 | tf_op jit(solution)/shard_map/ppermute | solution.py:404
  26.2 1.5 %collective-permute-start.8 = (f32[160,128]{1,0:T(8,128)S(1)}, f32[160,128]{1,0:T(8,128)S(1)}, u32[]{:S(2)}, u32[]{:S(2)}) collective-permute-start(f32[160,128]{1,0:T(8,128)S(1)} %add_add_fusion.refs_0_), channel_id=1, source_target_pairs={{0,4},{1,5},{2,6},{3,7},{4,0},{5,1},{6,2},{7,3},{8,12},{9,13},{10,... | collective-permute-start | bytes 245768 | tf_op jit(solution)/shard_map/ppermute | solution.py:404
  27.7 1.2 %collective-permute-start.7 = (f32[160,128]{1,0:T(8,128)S(1)}, f32[160,128]{1,0:T(8,128)S(1)}, u32[]{:S(2)}, u32[]{:S(2)}) collective-permute-start(f32[160,128]{1,0:T(8,128)S(1)} %add_add_fusion.refs_0_), channel_id=1, source_target_pairs={{0,2},{1,3},{2,0},{3,1},{4,6},{5,7},{6,4},{7,5},{8,10},{9,11},{10,... | collective-permute-start | bytes 245768 | tf_op jit(solution)/shard_map/ppermute | solution.py:404
  28.9 0.0 collective-permute-start.10
  28.9 2.1 %collective-permute-done.9.refs_3_ = f32[160,128]{1,0:T(8,128)S(1)} collective-permute-done((f32[160,128]{1,0:T(8,128)S(1)}, f32[160,128]{1,0:T(8,128)S(1)}, u32[]{:S(2)}, u32[]{:S(2)}) %collective-permute-start.9) | collective-permute-done | bytes 81952 | tf_op jit(solution)/shard_map/ppermute | solution.py:404
  31.0 0.0 collective-permute-start.13
  31.0 0.6 %collective-permute-done.8.refs_2_ = f32[160,128]{1,0:T(8,128)S(1)} collective-permute-done((f32[160,128]{1,0:T(8,128)S(1)}, f32[160,128]{1,0:T(8,128)S(1)}, u32[]{:S(2)}, u32[]{:S(2)}) %collective-permute-start.8) | collective-permute-done | bytes 81952 | tf_op jit(solution)/shard_map/ppermute | solution.py:404
  31.6 0.0 collective-permute-start.12
  31.6 0.6 %collective-permute-done.7.refs_1_ = f32[160,128]{1,0:T(8,128)S(1)} collective-permute-done((f32[160,128]{1,0:T(8,128)S(1)}, f32[160,128]{1,0:T(8,128)S(1)}, u32[]{:S(2)}, u32[]{:S(2)}) %collective-permute-start.7) | collective-permute-done | bytes 81952 | tf_op jit(solution)/shard_map/ppermute | solution.py:404
  32.1 0.0 collective-permute-start.11
  32.2 0.0 copy-done.1
  32.2 0.1 copy.6.refs_9_
  32.3 0.0 collective-permute-done.10.refs_4_
  32.3 0.0 collective-permute-done.13.refs_7_
  32.3 0.6 %collective-permute-done.12.refs_6_ = f32[160,128]{1,0:T(8,128)S(1)} collective-permute-done((f32[160,128]{1,0:T(8,128)S(1)}, f32[160,128]{1,0:T(8,128)S(1)}, u32[]{:S(2)}, u32[]{:S(2)}) %collective-permute-start.12) | collective-permute-done | bytes 81952 | tf_op jit(solution)/shard_map/ppermute | solution.py:404
  32.8 0.6 %collective-permute-done.11.refs_5_ = f32[160,128]{1,0:T(8,128)S(1)} collective-permute-done((f32[160,128]{1,0:T(8,128)S(1)}, f32[160,128]{1,0:T(8,128)S(1)}, u32[]{:S(2)}, u32[]{:S(2)}) %collective-permute-start.11) | collective-permute-done | bytes 81952 | tf_op jit(solution)/shard_map/ppermute | solution.py:404
  33.4 18.5 %factor_fit.1 = (f32[512,512]{1,0:T(8,128)}, f32[64,512]{1,0:T(8,128)}, f32[512,512]{1,0:T(8,128)}, f32[1,512]{1,0:T(1,128)}) custom-call(f32[160,128]{1,0:T(8,128)S(1)} %add_add_fusion.refs_0_, f32[160,128]{1,0:T(8,128)S(1)} %collective-permute-done.7.refs_1_, f32[160,128]{1,0:T(8,128)S(1)} %collective-permute-done.8.refs_2_, ...), custom_call_target="tpu_custom_call" | custom-call | tf_op jit(solution)/shard_map/factor_fit/pallas_call | solution.py:315
  (3 shorter events, 0.1 us)
Async XLA Ops:
  0.6 1.2 %copy-start = (f32[512,512]{1,0:T(8,128)S(1)}, f32[512,512]{1,0:T(8,128)}, u32[]{:S(2)}) copy-start(f32[512,512]{1,0:T(8,128)} %x_hbm.1) | copy-start | bytes 3145732
  4.1 1.8 %collective-permute-start = (f32[640,128]{1,0:T(8,128)S(1)}, f32[640,128]{1,0:T(8,128)S(1)}, u32[]{:S(2)}, u32[]{:S(2)}) collective-permute-start(f32[640,128]{1,0:T(8,128)S(1)} %get-tuple-element.16), channel_id=1, source_target_pairs={{0,1},{1,0},{2,3},{3,2},{4,5},{5,4},{6,7},{7,6},{8,9},{9,8},{10,11... | collective-permute-start | bytes 983048 | tf_op jit(solution)/shard_map/ppermute | solution.py:404
  5.9 5.7 %collective-permute-start.1 = (f32[160,128]{1,0:T(8,128)S(1)}, f32[160,128]{1,0:T(8,128)S(1)}, u32[]{:S(2)}, u32[]{:S(2)}) collective-permute-start(f32[160,128]{1,0:T(8,128)S(1)} %get-tuple-element.18), channel_id=1, source_target_pairs={{0,2},{1,3},{2,0},{3,1},{4,6},{5,7},{6,4},{7,5},{8,10},{9,11},{10,... | collective-permute-start | bytes 245768 | tf_op jit(solution)/shard_map/ppermute | solution.py:404
  8.8 5.3 %collective-permute-start.2 = (f32[160,128]{1,0:T(8,128)S(1)}, f32[160,128]{1,0:T(8,128)S(1)}, u32[]{:S(2)}, u32[]{:S(2)}) collective-permute-start(f32[160,128]{1,0:T(8,128)S(1)} %get-tuple-element.19), channel_id=1, source_target_pairs={{0,4},{1,5},{2,6},{3,7},{4,0},{5,1},{6,2},{7,3},{8,12},{9,13},{10,... | collective-permute-start | bytes 245768 | tf_op jit(solution)/shard_map/ppermute | solution.py:404
  10.4 5.3 %collective-permute-start.3 = (f32[160,128]{1,0:T(8,128)S(1)}, f32[160,128]{1,0:T(8,128)S(1)}, u32[]{:S(2)}, u32[]{:S(2)}) collective-permute-start(f32[160,128]{1,0:T(8,128)S(1)} %get-tuple-element.20), channel_id=1, source_target_pairs={{0,6},{1,7},{2,4},{3,5},{4,2},{5,3},{6,0},{7,1},{8,14},{9,15},{10,... | collective-permute-start | bytes 245768 | tf_op jit(solution)/shard_map/ppermute | solution.py:404
  15.7 6.3 %collective-permute-start.6 = (f32[160,128]{1,0:T(8,128)S(1)}, f32[160,128]{1,0:T(8,128)S(1)}, u32[]{:S(2)}, u32[]{:S(2)}) collective-permute-start(f32[160,128]{1,0:T(8,128)S(1)} %add_add_fusion.1), channel_id=1, source_target_pairs={{0,24},{1,25},{2,26},{3,27},{4,28},{5,29},{6,30},{7,31},{8,16},{9,... | collective-permute-start | bytes 245768 | tf_op jit(solution)/shard_map/ppermute | solution.py:404
  19.4 5.9 %collective-permute-start.5 = (f32[160,128]{1,0:T(8,128)S(1)}, f32[160,128]{1,0:T(8,128)S(1)}, u32[]{:S(2)}, u32[]{:S(2)}) collective-permute-start(f32[160,128]{1,0:T(8,128)S(1)} %add_add_fusion.1), channel_id=1, source_target_pairs={{0,16},{1,17},{2,18},{3,19},{4,20},{5,21},{6,22},{7,23},{8,24},{9,... | collective-permute-start | bytes 245768 | tf_op jit(solution)/shard_map/ppermute | solution.py:404
  19.4 5.9 %collective-permute-start.4 = (f32[160,128]{1,0:T(8,128)S(1)}, f32[160,128]{1,0:T(8,128)S(1)}, u32[]{:S(2)}, u32[]{:S(2)}) collective-permute-start(f32[160,128]{1,0:T(8,128)S(1)} %add_add_fusion.1), channel_id=1, source_target_pairs={{0,8},{1,9},{2,10},{3,11},{4,12},{5,13},{6,14},{7,15},{8,0},{9,1},... | collective-permute-start | bytes 245768 | tf_op jit(solution)/shard_map/ppermute | solution.py:404
  25.3 6.8 %copy-start.1 = (s32[64]{0:T(128)S(1)}, s32[64]{0:T(128)}, u32[]{:S(2)}) copy-start(s32[64]{0:T(128)} %param.3) | copy-start | bytes 772
  25.3 5.7 %collective-permute-start.9 = (f32[160,128]{1,0:T(8,128)S(1)}, f32[160,128]{1,0:T(8,128)S(1)}, u32[]{:S(2)}, u32[]{:S(2)}) collective-permute-start(f32[160,128]{1,0:T(8,128)S(1)} %add_add_fusion.refs_0_), channel_id=1, source_target_pairs={{0,6},{1,7},{2,4},{3,5},{4,2},{5,3},{6,0},{7,1},{8,14},{9,15},{10,... | collective-permute-start | bytes 245768 | tf_op jit(solution)/shard_map/ppermute | solution.py:404
  26.2 5.3 %collective-permute-start.8 = (f32[160,128]{1,0:T(8,128)S(1)}, f32[160,128]{1,0:T(8,128)S(1)}, u32[]{:S(2)}, u32[]{:S(2)}) collective-permute-start(f32[160,128]{1,0:T(8,128)S(1)} %add_add_fusion.refs_0_), channel_id=1, source_target_pairs={{0,4},{1,5},{2,6},{3,7},{4,0},{5,1},{6,2},{7,3},{8,12},{9,13},{10,... | collective-permute-start | bytes 245768 | tf_op jit(solution)/shard_map/ppermute | solution.py:404
  27.7 4.4 %collective-permute-start.7 = (f32[160,128]{1,0:T(8,128)S(1)}, f32[160,128]{1,0:T(8,128)S(1)}, u32[]{:S(2)}, u32[]{:S(2)}) collective-permute-start(f32[160,128]{1,0:T(8,128)S(1)} %add_add_fusion.refs_0_), channel_id=1, source_target_pairs={{0,2},{1,3},{2,0},{3,1},{4,6},{5,7},{6,4},{7,5},{8,10},{9,11},{10,... | collective-permute-start | bytes 245768 | tf_op jit(solution)/shard_map/ppermute | solution.py:404
  28.9 3.4 %collective-permute-start.10 = (f32[160,128]{1,0:T(8,128)S(1)}, f32[160,128]{1,0:T(8,128)S(1)}, u32[]{:S(2)}, u32[]{:S(2)}) collective-permute-start(f32[160,128]{1,0:T(8,128)S(1)} %add_add_fusion.refs_0_), channel_id=1, source_target_pairs={{0,1},{1,0},{2,3},{3,2},{4,5},{5,4},{6,7},{7,6},{8,9},{9,8},{10,11... | collective-permute-start | bytes 245768 | tf_op jit(solution)/shard_map/ppermute | solution.py:404
  31.0 1.3 %collective-permute-start.13 = (f32[160,128]{1,0:T(8,128)S(1)}, f32[160,128]{1,0:T(8,128)S(1)}, u32[]{:S(2)}, u32[]{:S(2)}) collective-permute-start(f32[160,128]{1,0:T(8,128)S(1)} %collective-permute-done.9.refs_3_), channel_id=1, source_target_pairs={{0,1},{1,0},{2,3},{3,2},{4,5},{5,4},{6,7},{7,6},{8,9},{9,8},{10,11... | collective-permute-start | bytes 245768 | tf_op jit(solution)/shard_map/ppermute | solution.py:404
  31.6 1.3 %collective-permute-start.12 = (f32[160,128]{1,0:T(8,128)S(1)}, f32[160,128]{1,0:T(8,128)S(1)}, u32[]{:S(2)}, u32[]{:S(2)}) collective-permute-start(f32[160,128]{1,0:T(8,128)S(1)} %collective-permute-done.8.refs_2_), channel_id=1, source_target_pairs={{0,1},{1,0},{2,3},{3,2},{4,5},{5,4},{6,7},{7,6},{8,9},{9,8},{10,11... | collective-permute-start | bytes 245768 | tf_op jit(solution)/shard_map/ppermute | solution.py:404
  32.1 1.3 %collective-permute-start.11 = (f32[160,128]{1,0:T(8,128)S(1)}, f32[160,128]{1,0:T(8,128)S(1)}, u32[]{:S(2)}, u32[]{:S(2)}) collective-permute-start(f32[160,128]{1,0:T(8,128)S(1)} %collective-permute-done.7.refs_1_), channel_id=1, source_target_pairs={{0,1},{1,0},{2,3},{3,2},{4,5},{5,4},{6,7},{7,6},{8,9},{9,8},{10,11... | collective-permute-start | bytes 245768 | tf_op jit(solution)/shard_map/ppermute | solution.py:404
where the time goes:
time: 52.3 us; the launch traced here: 52.1 us
  Pallas kernels  20.8 us (40%)
  waiting for transfers between devices  16.1 us (31%)
  starting transfers between devices  13 us (25%)
  local copies, waits for them, and re-layouts  1.32 us (3%)
  between operations  0.84 us (2%)
    pallas_call x1, Pallas kernels, fit_call(): pl.pallas_call(body, out_shape=(jax.ShapeDtypeStruct((512, 512), f32), ja...  18.5 us
    ppermute x14, waiting for transfers between devices, swap(): return lax.ppermute(x, AXES, [(i, i ^ bit) for i in range(devices)])  16.1 us
    ppermute x14, starting transfers between devices, swap(): return lax.ppermute(x, AXES, [(i, i ^ bit) for i in range(devices)])  13 us
    pallas_call x1, Pallas kernels, gram_call(): pl.pallas_call(gram_kernel, out_shape=(half, half, jax.ShapeDtypeStruct(x...  2.24 us
    unnamed x4, local copies, waits for them, and re-layouts  1.22 us
  transfers between devices with their start and end apart: 14, of which 11 were waited for; matrix products, arithmetic and copies ran while one was open for 0% of the time, Pallas kernels for 0%

commit v1 on v0

--- a/solution.py
+++ b/solution.py
@@ -12,6 +12,8 @@
 NT = (((1,), (1,)), ((), ()))
 TN = (((0,), (0,)), ((), ()))
 PANEL = 32
+HALF = 576
+PIECE = HALF // 4
 LEFT = (0, 0, 1, 0, 2, 1)
 RIGHT = (0, 1, 0, 2, 0, 1)
 
@@ -131,54 +133,121 @@
 
 def cholesky_steps(t_ref, e_ref, s_ref, size, blocks, done):
     later = []
+    steps = PANEL // 8
+
+    def apply(inverse, rows, c0, width, both):
+        at = slice(c0 + 128, c0 + 128 * width)
+        parts = ([t_ref[rows, at]] if width > 1 else []) + ([e_ref[rows, :]] if both else [])
+        if not parts:
+            return
+        x = lax.dot_general(
+            inverse,
+            jnp.concatenate(parts, axis=1),
+            NN,
+            precision=lax.Precision.HIGHEST,
+            preferred_element_type=jnp.float32,
+        )
+        if width > 1:
+            t_ref[rows, at] = x[:, : 128 * (width - 1)]
+        if both:
+            e_ref[rows, :] = x[:, 128 * (width - 1) :]
+
+    def sides(x):
+        split = thirds(x)
+        left = jnp.concatenate([split[i] for i in LEFT], axis=0).T
+        return left, jnp.concatenate([split[i] for i in RIGHT], axis=0)
+
+    def update(ref, rows, at, left, right):
+        ref[rows, at] = ref[rows, at] - bdot(left, right, NN)
+
     for k in range(blocks):
-        r0, c0 = k * size, k * 128
+        r0, c0, width = k * size, k * 128, blocks - k
         e_ref[r0 : r0 + size, :] = eye(size, 128)
+        here = slice(c0, c0 + 128)
         for p in range(size // PANEL):
             base = r0 + p * PANEL
-            width = blocks - k
+            rows = slice(base, base + PANEL)
             tiles = []
-            for t in range(PANEL // 8):
-                at = slice(base + 8 * t, base + 8 * t + 8)
-                tiles.append(
-                    [t_ref[at, c0 + 128 * w : c0 + 128 * w + 128] for w in range(width)] + [e_ref[at, :]]
-                )
+            unit = eye(PANEL, 128)
+            for t in range(steps):
+                tiles.append([t_ref[base + 8 * t : base + 8 * t + 8, here], unit[8 * t : 8 * t + 8, :]])
             outs = []
-            steps = PANEL // 8
             for t in range(steps):
                 out, tiles = eliminate(tiles, p * PANEL + 8 * t, s_ref.at[(p * steps + t) % 8])
                 outs.append(out)
                 for _ in range(-(-len(later) // (steps - t))):
                     later.pop(0)()
                 yield
-            full = [jnp.concatenate([o[w] for o in outs], axis=0) for w in range(width + 1)]
-            for w in range(width):
-                t_ref[base : base + PANEL, c0 + 128 * w : c0 + 128 * w + 128] = full[w]
-            e_ref[base : base + PANEL, :] = full[width]
-            split = [thirds(x) for x in full]
-            left = [jnp.concatenate([s[i] for i in LEFT], axis=0) for s in split]
-            right = [jnp.concatenate([s[i] for i in RIGHT], axis=0) for s in split]
-            last = base + PANEL == r0 + size
-
-            def update(w, lo, hi, flip, r0=r0, c0=c0, width=width, right=right):
-                both = bdot(flip[lo:hi], jnp.concatenate(right[w:] if w == 0 else right[w:width], axis=1), NN)
-                rows = slice(r0 + size * w + lo, r0 + size * w + hi)
-                at = slice(c0 + 128 * w, c0 + 128 * width)
-                t_ref[rows, at] = t_ref[rows, at] - both[:, : 128 * (width - w)]
-                if w == 0:
-                    e_ref[rows, :] = e_ref[rows, :] - both[:, 128 * width :]
-
-            for w in range(1 if last else 0, width):
-                lo = 0 if w else (p + 1) * PANEL
-                flip = left[w].T
-                first = w == (1 if last else 0)
-                if first:
-                    update(w, lo, lo + PANEL, flip)
-                    lo += PANEL
-                if lo < size:
-                    later.append(functools.partial(update, w, lo, size, flip))
+            up = jnp.concatenate([o[0] for o in outs], axis=0)
+            inverse = jnp.concatenate([o[1] for o in outs], axis=0)[:, :PANEL]
+            t_ref[rows, here] = up
+            nxt = (p + 1) * PANEL
+            last = nxt == size
+            if not last:
+                left, right = sides(up)
+                update(t_ref, slice(base + PANEL, base + 2 * PANEL), here, left[nxt : nxt + PANEL], right)
+                if nxt + PANEL < size:
+                    later.append(
+                        functools.partial(
+                            update, t_ref, slice(base + 2 * PANEL, r0 + size), here, left[nxt + PANEL : size], right
+                        )
+                    )
+
+            def others(left=None, rows=rows, r0=r0, c0=c0, width=width, nxt=nxt, inverse=inverse):
+                cols = slice(c0 + 128, c0 + 128 * width)
+                w_left, w_right = [], []
+                for w in range(1, width):
+                    a, b = sides(t_ref[rows, c0 + 128 * w : c0 + 128 * w + 128])
+                    w_left.append(a)
+                    w_right.append(b)
+                if left is not None:
+                    e_left, e_right = sides(e_ref[rows, :])
+                    in_block = slice(r0 + nxt, r0 + size)
+                    if width > 1:
+                        update(t_ref, in_block, cols, left[nxt:size], jnp.concatenate(w_right, axis=1))
+                    update(e_ref, in_block, slice(0, 128), left[nxt:size], e_right)
+                return w_left, w_right
+
+            def below(w_left, w_right, r0=r0, c0=c0, width=width, skip=False):
+                for w in range(1, width):
+                    at = slice(c0 + 128 * w, c0 + 128 * width)
+                    lo = 0
+                    right = jnp.concatenate(w_right[w - 1 :], axis=1)
+                    if w == 1 and skip:
+                        first = slice(r0 + size, r0 + size + PANEL)
+                        if width > 2:
+                            update(t_ref, first, slice(at.start + 128, at.stop), w_left[0][:PANEL], right[:, 128:])
+                        lo = PANEL
+                    update(t_ref, slice(r0 + size * w + lo, r0 + size * w + size), at, w_left[w - 1][lo:size], right)
+
             if last:
+                apply(inverse, rows, c0, width, True)
+                if width > 1:
+                    w_left, w_right = others()
+                    update(
+                        t_ref,
+                        slice(r0 + size, r0 + size + PANEL),
+                        slice(c0 + 128, c0 + 256),
+                        w_left[0][:PANEL],
+                        w_right[0],
+                    )
+                    later.append(functools.partial(below, w_left, w_right, skip=True))
                 done(k)
+            else:
+
+                def second(
+                    left=left, others=others, below=below, inverse=inverse, rows=rows, c0=c0, width=width
+                ):
+                    apply(inverse, rows, c0, width, True)
+                    held.append(others(left))
+
+                def third(below=below):
+                    below(*held.pop(0))
+
+                held = []
+                later.append(second)
+                if width > 1:
+                    later.append(third)
 
 
 def main_kernel(total, pieces, data_ref, anc_ref, fac_out, coef_out, bas_out, res_out, t_ref, e_ref, y_ref, f_ref, td_ref, ed_ref, rk_ref, cf_ref, sq_ref, s_ref, g_ref, sem):
@@ -201,7 +270,12 @@
         sums = [None] * nb
         for i in range(nb):
             for j in range(i, nb):
-                g = thirds(state["gram"][i, j])
+                whole = state["gram"][i, j]
+                if i == j:
+                    r = lax.broadcasted_iota(jnp.int32, (128, 128), 0)
+                    c = lax.broadcasted_iota(jnp.int32, (128, 128), 1)
+                    whole = jnp.where((r >= 64) & (c < 64), whole.T, whole)
+                g = thirds(whole)
                 pi, pj = pick[:, 128 * i : 128 * i + 128], pick[:, 128 * j : 128 * j + 128]
                 for x in g:
                     v = bdot(pi, x, NN)
@@ -292,14 +366,21 @@
     me = my_index()
     core, q = lax.rem(me, 2), lax.rem(me // 2, 4)
     for m in range(8):
-        at = (core ^ (m // 4)) * 640 + (q ^ (m % 4)) * 160
-        g_ref[pl.ds(pl.multiple_of(at, 160), 160), :] = pieces[m][...]
+        at = (core ^ (m // 4)) * HALF + (q ^ (m % 4)) * PIECE
+        g_ref[pl.ds(pl.multiple_of(at, PIECE), PIECE), :] = pieces[m][...] / total
     n = 0
     for i in range(4):
-        for j in range(i, 4):
-            x = g_ref[128 * n : 128 * n + 128, :] / total
-            t_ref[128 * i : 128 * i + 128, 128 * j : 128 * j + 128] = x
-            n += 1
+        rows = slice(128 * i, 128 * i + 64)
+        t_ref[rows, 128 * i : 128 * i + 128] = g_ref[64 * n : 64 * n + 64, :]
+        n += 1
+        for j in range(i + 1, 4):
+            t_ref[128 * i : 128 * i + 128, 128 * j : 128 * j + 128] = g_ref[64 * n : 64 * n + 128, :]
+            n += 2
+    for i in range(4):
+        x = g_ref[64 * (n + i // 2) : 64 * (n + i // 2) + 64, :]
+        if i % 2 == 0:
+            x = pltpu.roll(x, 64, 1)
+        t_ref[128 * i + 64 : 128 * i + 128, 128 * i : 128 * i + 128] = x
 
 
 def fit_call(pieces, data, anchors, total):
@@ -333,7 +414,7 @@
             pltpu.VMEM((64, 512), f32),
             pltpu.VMEM((1, 512), f32),
             pltpu.VMEM((2, 8, 64, 128), f32),
-            pltpu.VMEM((1280, 128), f32),
+            pltpu.VMEM((2 * HALF, 128), f32),
             pltpu.SemaphoreType.DMA((10,)),
         ],
         compiler_params=pltpu.CompilerParams(vmem_limit_bytes=32 << 20),
@@ -352,46 +433,55 @@
         at = pl.ds(rows * c, rows)
         copies.append(pltpu.make_async_copy(x_hbm.at[at, :], x_ref.at[at, :], sem.at[c]))
         copies[-1].start()
-    for c in range(4):
-        copies[c].wait()
-        split = thirds(x_ref[rows * c : rows * c + rows, :])
-        left = jnp.concatenate([split[i] for i in LEFT], axis=0)
-        right = jnp.concatenate([split[i] for i in RIGHT], axis=0)
-        n = 0
-        for i in range(4):
-            row = bdot(left[:, 128 * i : 128 * i + 128], right[:, 128 * i :], TN)
-            for j in range(4 - i):
-                at = slice(128 * (n % 5), 128 * (n % 5) + 128)
-                x = row[:, 128 * j : 128 * j + 128]
-                both_ref[n // 5, at, :] = x if c == 0 else both_ref[n // 5, at, :] + x
+    for c in copies:
+        c.wait()
+    x = x_ref[...]
+
+    def put(n, unit):
+        both_ref[n // 9, 64 * (n % 9) : 64 * (n % 9) + 64, :] = unit
+
+    n = 0
+    corners = []
+    for i in range(4):
+        row = mm(x[:, 128 * i : 128 * i + 128], x[:, 128 * i :], TN)
+        for j in range(4 - i):
+            put(n, row[:64, 128 * j : 128 * j + 128])
+            n += 1
+            if j:
+                put(n, row[64:, 128 * j : 128 * j + 128])
                 n += 1
+        corners.append(row[64:, :128])
+    lanes = lax.broadcasted_iota(jnp.int32, (64, 128), 1)
+    for i in (0, 2):
+        put(n, jnp.where(lanes < 64, pltpu.roll(corners[i], 64, 1), corners[i + 1]))
+        n += 1
     bit = lax.rem(my_index(), 2)
     own_ref[...] = both_ref[bit]
     other_ref[...] = both_ref[1 - bit]
 
 
 def gram_call(x):
-    half = jax.ShapeDtypeStruct((640, 128), jnp.float32)
+    half = jax.ShapeDtypeStruct((HALF, 128), jnp.float32)
     return pl.pallas_call(
         gram_kernel,
         out_shape=(half, half, jax.ShapeDtypeStruct(x.shape, x.dtype)),
         in_specs=[pl.BlockSpec(memory_space=pltpu.HBM)],
         out_specs=(pl.BlockSpec(memory_space=pltpu.VMEM),) * 3,
-        scratch_shapes=[pltpu.VMEM((2, 640, 128), jnp.float32), pltpu.SemaphoreType.DMA((4,))],
+        scratch_shapes=[pltpu.VMEM((2, HALF, 128), jnp.float32), pltpu.SemaphoreType.DMA((4,))],
         compiler_params=pltpu.CompilerParams(vmem_limit_bytes=16 << 20),
         name="gram",
-    )(x)
+    )(pltpu.with_memory_space_constraint(x, pltpu.HBM))
 
 
 def split_kernel(own_ref, got_ref, *outs):
     q = lax.rem(my_index() // 2, 4)
     for m, out in enumerate(outs):
-        rows = pl.ds(pl.multiple_of((q ^ m) * 160, 160), 160)
+        rows = pl.ds(pl.multiple_of((q ^ m) * PIECE, PIECE), PIECE)
         out[...] = own_ref[rows, :] + got_ref[rows, :]
 
 
 def split_call(own, got):
-    part = jax.ShapeDtypeStruct((160, 128), jnp.float32)
+    part = jax.ShapeDtypeStruct((PIECE, 128), jnp.float32)
     return pl.pallas_call(
         split_kernel,
         out_shape=(part,) * 4,

time: 52.3 us -> 50.7 us (0.969)
  local copies, waits for them, and re-layouts: 1.32 us -> 0.1 us
  waiting for transfers between devices: 16.1 us -> 15.2 us
  Pallas kernels: 20.8 us -> 21.4 us
    unnamed x4 -> x2, local copies, waits for them, and re-layouts: 1.22 us -> 0.01 us
    ppermute x14, waiting for transfers between devices: 16.1 us -> 15.2 us  [swap(): return lax.ppermute(x, AXES, [(i, i ^ bit) for i in range(devices)])]
    pallas_call x1, Pallas kernels: 2.24 us -> 2.81 us  [gram_call(): pl.pallas_call(gram_kernel, out_shape=(half, half, jax.ShapeDtypeStruct(x...]
where the time goes in v1:
time: 50.7 us; the launch traced here: 50.5 us
  Pallas kernels  21.4 us (42%)
  waiting for transfers between devices  15.2 us (30%)
  starting transfers between devices  13 us (26%)
  between operations  0.84 us (2%)
    pallas_call x1, Pallas kernels, fit_call(): pl.pallas_call(body, out_shape=(jax.ShapeDtypeStruct((512, 512), f32), ja...  18.5 us
    ppermute x14, waiting for transfers between devices, swap(): return lax.ppermute(x, AXES, [(i, i ^ bit) for i in range(devices)])  15.2 us
    ppermute x14, starting transfers between devices, swap(): return lax.ppermute(x, AXES, [(i, i ^ bit) for i in range(devices)])  13 us
    pallas_call x1, Pallas kernels, gram_call(): pl.pallas_call(gram_kernel, out_shape=(half, half, jax.ShapeDtypeStruct(x...  2.81 us
  transfers between devices with their start and end apart: 14, of which 11 were waited for; matrix products, arithmetic and copies ran while one was open for 0% of the time, Pallas kernels for 0%

profile of v1, /device:TPU:0, one launch (start us, length us, event | category | flops | bytes accessed | tf_op | source)
XLA Modules:
  0.0 50.5 jit_solution(9282382074179386173)
XLA Ops:
  0.6 2.8 %gram.1 = (f32[576,128]{1,0:T(8,128)S(1)}, f32[576,128]{1,0:T(8,128)S(1)}, f32[512,512]{1,0:T(8,128)S(1)}) custom-call(f32[512,512]{1,0:T(8,128)} %x_hbm.1), custom_call_target="tpu_custom_call" | custom-call | tf_op jit(solution)/shard_map/gram/pallas_call | solution.py:465
  3.4 0.5 %collective-permute-start = (f32[576,128]{1,0:T(8,128)S(1)}, f32[576,128]{1,0:T(8,128)S(1)}, u32[]{:S(2)}, u32[]{:S(2)}) collective-permute-start(f32[576,128]{1,0:T(8,128)S(1)} %get-tuple-element.16), channel_id=1, source_target_pairs={{0,1},{1,0},{2,3},{3,2},{4,5},{5,4},{6,7},{7,6},{8,9},{9,8},{10,11... | collective-permute-start | bytes 884744 | tf_op jit(solution)/shard_map/ppermute | solution.py:494
  4.0 1.2 %collective-permute-done.got_ref = f32[576,128]{1,0:T(8,128)S(1)} collective-permute-done((f32[576,128]{1,0:T(8,128)S(1)}, f32[576,128]{1,0:T(8,128)S(1)}, u32[]{:S(2)}, u32[]{:S(2)}) %collective-permute-start) | collective-permute-done | bytes 294944 | tf_op jit(solution)/shard_map/ppermute | solution.py:494
  5.2 2.9 %collective-permute-start.1 = (f32[144,128]{1,0:T(8,128)S(1)}, f32[144,128]{1,0:T(8,128)S(1)}, u32[]{:S(2)}, u32[]{:S(2)}) collective-permute-start(f32[144,128]{1,0:T(8,128)S(1)} %get-tuple-element.18), channel_id=1, source_target_pairs={{0,2},{1,3},{2,0},{3,1},{4,6},{5,7},{6,4},{7,5},{8,10},{9,11},{10,... | collective-permute-start | bytes 221192 | tf_op jit(solution)/shard_map/ppermute | solution.py:494
  8.1 1.5 %collective-permute-start.2 = (f32[144,128]{1,0:T(8,128)S(1)}, f32[144,128]{1,0:T(8,128)S(1)}, u32[]{:S(2)}, u32[]{:S(2)}) collective-permute-start(f32[144,128]{1,0:T(8,128)S(1)} %get-tuple-element.19), channel_id=1, source_target_pairs={{0,4},{1,5},{2,6},{3,7},{4,0},{5,1},{6,2},{7,3},{8,12},{9,13},{10,... | collective-permute-start | bytes 221192 | tf_op jit(solution)/shard_map/ppermute | solution.py:494
  9.7 0.0 collective-permute-start.3
  9.7 1.0 %collective-permute-done.1 = f32[144,128]{1,0:T(8,128)S(1)} collective-permute-done((f32[144,128]{1,0:T(8,128)S(1)}, f32[144,128]{1,0:T(8,128)S(1)}, u32[]{:S(2)}, u32[]{:S(2)}) %collective-permute-start.1) | collective-permute-done | bytes 73760 | tf_op jit(solution)/shard_map/ppermute | solution.py:494
  10.7 1.8 %collective-permute-done.2 = f32[144,128]{1,0:T(8,128)S(1)} collective-permute-done((f32[144,128]{1,0:T(8,128)S(1)}, f32[144,128]{1,0:T(8,128)S(1)}, u32[]{:S(2)}, u32[]{:S(2)}) %collective-permute-start.2) | collective-permute-done | bytes 73760 | tf_op jit(solution)/shard_map/ppermute | solution.py:494
  12.5 2.4 %collective-permute-done.3 = f32[144,128]{1,0:T(8,128)S(1)} collective-permute-done((f32[144,128]{1,0:T(8,128)S(1)}, f32[144,128]{1,0:T(8,128)S(1)}, u32[]{:S(2)}, u32[]{:S(2)}) %collective-permute-start.3) | collective-permute-done | bytes 73760 | tf_op jit(solution)/shard_map/ppermute | solution.py:494
  14.9 3.7 %collective-permute-start.6 = (f32[144,128]{1,0:T(8,128)S(1)}, f32[144,128]{1,0:T(8,128)S(1)}, u32[]{:S(2)}, u32[]{:S(2)}) collective-permute-start(f32[144,128]{1,0:T(8,128)S(1)} %add_add_fusion.1), channel_id=1, source_target_pairs={{0,24},{1,25},{2,26},{3,27},{4,28},{5,29},{6,30},{7,31},{8,16},{9,... | collective-permute-start | bytes 221192 | tf_op jit(solution)/shard_map/ppermute | solution.py:494
  18.6 0.0 collective-permute-start.5
  18.6 0.8 %collective-permute-start.4 = (f32[144,128]{1,0:T(8,128)S(1)}, f32[144,128]{1,0:T(8,128)S(1)}, u32[]{:S(2)}, u32[]{:S(2)}) collective-permute-start(f32[144,128]{1,0:T(8,128)S(1)} %add_add_fusion.1), channel_id=1, source_target_pairs={{0,8},{1,9},{2,10},{3,11},{4,12},{5,13},{6,14},{7,15},{8,0},{9,1},... | collective-permute-start | bytes 221192 | tf_op jit(solution)/shard_map/ppermute | solution.py:494
  19.4 1.8 %collective-permute-done.6 = f32[144,128]{1,0:T(8,128)S(1)} collective-permute-done((f32[144,128]{1,0:T(8,128)S(1)}, f32[144,128]{1,0:T(8,128)S(1)}, u32[]{:S(2)}, u32[]{:S(2)}) %collective-permute-start.6) | collective-permute-done | bytes 73760 | tf_op jit(solution)/shard_map/ppermute | solution.py:494
  21.2 2.8 %collective-permute-done.5 = f32[144,128]{1,0:T(8,128)S(1)} collective-permute-done((f32[144,128]{1,0:T(8,128)S(1)}, f32[144,128]{1,0:T(8,128)S(1)}, u32[]{:S(2)}, u32[]{:S(2)}) %collective-permute-start.5) | collective-permute-done | bytes 73760 | tf_op jit(solution)/shard_map/ppermute | solution.py:494
  24.0 0.0 collective-permute-done.4
  24.0 0.0 copy-start
  24.0 0.8 %collective-permute-start.9 = (f32[144,128]{1,0:T(8,128)S(1)}, f32[144,128]{1,0:T(8,128)S(1)}, u32[]{:S(2)}, u32[]{:S(2)}) collective-permute-start(f32[144,128]{1,0:T(8,128)S(1)} %add_add_fusion.refs_0_), channel_id=1, source_target_pairs={{0,6},{1,7},{2,4},{3,5},{4,2},{5,3},{6,0},{7,1},{8,14},{9,15},{10,... | collective-permute-start | bytes 221192 | tf_op jit(solution)/shard_map/ppermute | solution.py:494
  24.8 1.5 %collective-permute-start.8 = (f32[144,128]{1,0:T(8,128)S(1)}, f32[144,128]{1,0:T(8,128)S(1)}, u32[]{:S(2)}, u32[]{:S(2)}) collective-permute-start(f32[144,128]{1,0:T(8,128)S(1)} %add_add_fusion.refs_0_), channel_id=1, source_target_pairs={{0,4},{1,5},{2,6},{3,7},{4,0},{5,1},{6,2},{7,3},{8,12},{9,13},{10,... | collective-permute-start | bytes 221192 | tf_op jit(solution)/shard_map/ppermute | solution.py:494
  26.3 1.3 %collective-permute-start.7 = (f32[144,128]{1,0:T(8,128)S(1)}, f32[144,128]{1,0:T(8,128)S(1)}, u32[]{:S(2)}, u32[]{:S(2)}) collective-permute-start(f32[144,128]{1,0:T(8,128)S(1)} %add_add_fusion.refs_0_), channel_id=1, source_target_pairs={{0,2},{1,3},{2,0},{3,1},{4,6},{5,7},{6,4},{7,5},{8,10},{9,11},{10,... | collective-permute-start | bytes 221192 | tf_op jit(solution)/shard_map/ppermute | solution.py:494
  27.6 0.0 collective-permute-start.10
  27.6 1.9 %collective-permute-done.9.refs_3_ = f32[144,128]{1,0:T(8,128)S(1)} collective-permute-done((f32[144,128]{1,0:T(8,128)S(1)}, f32[144,128]{1,0:T(8,128)S(1)}, u32[]{:S(2)}, u32[]{:S(2)}) %collective-permute-start.9) | collective-permute-done | bytes 73760 | tf_op jit(solution)/shard_map/ppermute | solution.py:494
  29.4 0.0 collective-permute-start.13
  29.4 0.5 collective-permute-done.8.refs_2_
  29.9 0.0 collective-permute-start.12
  29.9 0.7 %collective-permute-done.7.refs_1_ = f32[144,128]{1,0:T(8,128)S(1)} collective-permute-done((f32[144,128]{1,0:T(8,128)S(1)}, f32[144,128]{1,0:T(8,128)S(1)}, u32[]{:S(2)}, u32[]{:S(2)}) %collective-permute-start.7) | collective-permute-done | bytes 73760 | tf_op jit(solution)/shard_map/ppermute | solution.py:494
  30.6 0.0 collective-permute-start.11
  30.6 0.0 copy-done
  30.6 0.1 copy.6.refs_9_
  30.7 0.0 collective-permute-done.10.refs_4_
  30.7 0.0 collective-permute-done.13.refs_7_
  30.7 0.5 collective-permute-done.12.refs_6_
  31.2 0.7 %collective-permute-done.11.refs_5_ = f32[144,128]{1,0:T(8,128)S(1)} collective-permute-done((f32[144,128]{1,0:T(8,128)S(1)}, f32[144,128]{1,0:T(8,128)S(1)}, u32[]{:S(2)}, u32[]{:S(2)}) %collective-permute-start.11) | collective-permute-done | bytes 73760 | tf_op jit(solution)/shard_map/ppermute | solution.py:494
  31.9 18.5 %factor_fit.1 = (f32[512,512]{1,0:T(8,128)}, f32[64,512]{1,0:T(8,128)}, f32[512,512]{1,0:T(8,128)}, f32[1,512]{1,0:T(1,128)}) custom-call(f32[144,128]{1,0:T(8,128)S(1)} %add_add_fusion.refs_0_, f32[144,128]{1,0:T(8,128)S(1)} %collective-permute-done.7.refs_1_, f32[144,128]{1,0:T(8,128)S(1)} %collective-permute-done.8.refs_2_, ...), custom_call_target="tpu_custom_call" | custom-call | tf_op jit(solution)/shard_map/factor_fit/pallas_call | solution.py:396
  (3 shorter events, 0.1 us)
Async XLA Ops:
  3.4 1.7 %collective-permute-start = (f32[576,128]{1,0:T(8,128)S(1)}, f32[576,128]{1,0:T(8,128)S(1)}, u32[]{:S(2)}, u32[]{:S(2)}) collective-permute-start(f32[576,128]{1,0:T(8,128)S(1)} %get-tuple-element.16), channel_id=1, source_target_pairs={{0,1},{1,0},{2,3},{3,2},{4,5},{5,4},{6,7},{7,6},{8,9},{9,8},{10,11... | collective-permute-start | bytes 884744 | tf_op jit(solution)/shard_map/ppermute | solution.py:494
  5.2 5.5 %collective-permute-start.1 = (f32[144,128]{1,0:T(8,128)S(1)}, f32[144,128]{1,0:T(8,128)S(1)}, u32[]{:S(2)}, u32[]{:S(2)}) collective-permute-start(f32[144,128]{1,0:T(8,128)S(1)} %get-tuple-element.18), channel_id=1, source_target_pairs={{0,2},{1,3},{2,0},{3,1},{4,6},{5,7},{6,4},{7,5},{8,10},{9,11},{10,... | collective-permute-start | bytes 221192 | tf_op jit(solution)/shard_map/ppermute | solution.py:494
  8.1 4.4 %collective-permute-start.2 = (f32[144,128]{1,0:T(8,128)S(1)}, f32[144,128]{1,0:T(8,128)S(1)}, u32[]{:S(2)}, u32[]{:S(2)}) collective-permute-start(f32[144,128]{1,0:T(8,128)S(1)} %get-tuple-element.19), channel_id=1, source_target_pairs={{0,4},{1,5},{2,6},{3,7},{4,0},{5,1},{6,2},{7,3},{8,12},{9,13},{10,... | collective-permute-start | bytes 221192 | tf_op jit(solution)/shard_map/ppermute | solution.py:494
  9.7 5.3 %collective-permute-start.3 = (f32[144,128]{1,0:T(8,128)S(1)}, f32[144,128]{1,0:T(8,128)S(1)}, u32[]{:S(2)}, u32[]{:S(2)}) collective-permute-start(f32[144,128]{1,0:T(8,128)S(1)} %get-tuple-element.20), channel_id=1, source_target_pairs={{0,6},{1,7},{2,4},{3,5},{4,2},{5,3},{6,0},{7,1},{8,14},{9,15},{10,... | collective-permute-start | bytes 221192 | tf_op jit(solution)/shard_map/ppermute | solution.py:494
  14.9 6.2 %collective-permute-start.6 = (f32[144,128]{1,0:T(8,128)S(1)}, f32[144,128]{1,0:T(8,128)S(1)}, u32[]{:S(2)}, u32[]{:S(2)}) collective-permute-start(f32[144,128]{1,0:T(8,128)S(1)} %add_add_fusion.1), channel_id=1, source_target_pairs={{0,24},{1,25},{2,26},{3,27},{4,28},{5,29},{6,30},{7,31},{8,16},{9,... | collective-permute-start | bytes 221192 | tf_op jit(solution)/shard_map/ppermute | solution.py:494
  18.6 5.4 %collective-permute-start.5 = (f32[144,128]{1,0:T(8,128)S(1)}, f32[144,128]{1,0:T(8,128)S(1)}, u32[]{:S(2)}, u32[]{:S(2)}) collective-permute-start(f32[144,128]{1,0:T(8,128)S(1)} %add_add_fusion.1), channel_id=1, source_target_pairs={{0,16},{1,17},{2,18},{3,19},{4,20},{5,21},{6,22},{7,23},{8,24},{9,... | collective-permute-start | bytes 221192 | tf_op jit(solution)/shard_map/ppermute | solution.py:494
  18.6 5.4 %collective-permute-start.4 = (f32[144,128]{1,0:T(8,128)S(1)}, f32[144,128]{1,0:T(8,128)S(1)}, u32[]{:S(2)}, u32[]{:S(2)}) collective-permute-start(f32[144,128]{1,0:T(8,128)S(1)} %add_add_fusion.1), channel_id=1, source_target_pairs={{0,8},{1,9},{2,10},{3,11},{4,12},{5,13},{6,14},{7,15},{8,0},{9,1},... | collective-permute-start | bytes 221192 | tf_op jit(solution)/shard_map/ppermute | solution.py:494
  24.0 6.6 %copy-start = (s32[64]{0:T(128)S(1)}, s32[64]{0:T(128)}, u32[]{:S(2)}) copy-start(s32[64]{0:T(128)} %param.3) | copy-start | bytes 772
  24.0 5.4 %collective-permute-start.9 = (f32[144,128]{1,0:T(8,128)S(1)}, f32[144,128]{1,0:T(8,128)S(1)}, u32[]{:S(2)}, u32[]{:S(2)}) collective-permute-start(f32[144,128]{1,0:T(8,128)S(1)} %add_add_fusion.refs_0_), channel_id=1, source_target_pairs={{0,6},{1,7},{2,4},{3,5},{4,2},{5,3},{6,0},{7,1},{8,14},{9,15},{10,... | collective-permute-start | bytes 221192 | tf_op jit(solution)/shard_map/ppermute | solution.py:494
  24.8 5.1 %collective-permute-start.8 = (f32[144,128]{1,0:T(8,128)S(1)}, f32[144,128]{1,0:T(8,128)S(1)}, u32[]{:S(2)}, u32[]{:S(2)}) collective-permute-start(f32[144,128]{1,0:T(8,128)S(1)} %add_add_fusion.refs_0_), channel_id=1, source_target_pairs={{0,4},{1,5},{2,6},{3,7},{4,0},{5,1},{6,2},{7,3},{8,12},{9,13},{10,... | collective-permute-start | bytes 221192 | tf_op jit(solution)/shard_map/ppermute | solution.py:494
  26.3 4.4 %collective-permute-start.7 = (f32[144,128]{1,0:T(8,128)S(1)}, f32[144,128]{1,0:T(8,128)S(1)}, u32[]{:S(2)}, u32[]{:S(2)}) collective-permute-start(f32[144,128]{1,0:T(8,128)S(1)} %add_add_fusion.refs_0_), channel_id=1, source_target_pairs={{0,2},{1,3},{2,0},{3,1},{4,6},{5,7},{6,4},{7,5},{8,10},{9,11},{10,... | collective-permute-start | bytes 221192 | tf_op jit(solution)/shard_map/ppermute | solution.py:494
  27.6 3.1 %collective-permute-start.10 = (f32[144,128]{1,0:T(8,128)S(1)}, f32[144,128]{1,0:T(8,128)S(1)}, u32[]{:S(2)}, u32[]{:S(2)}) collective-permute-start(f32[144,128]{1,0:T(8,128)S(1)} %add_add_fusion.refs_0_), channel_id=1, source_target_pairs={{0,1},{1,0},{2,3},{3,2},{4,5},{5,4},{6,7},{7,6},{8,9},{9,8},{10,11... | collective-permute-start | bytes 221192 | tf_op jit(solution)/shard_map/ppermute | solution.py:494
  29.4 1.3 %collective-permute-start.13 = (f32[144,128]{1,0:T(8,128)S(1)}, f32[144,128]{1,0:T(8,128)S(1)}, u32[]{:S(2)}, u32[]{:S(2)}) collective-permute-start(f32[144,128]{1,0:T(8,128)S(1)} %collective-permute-done.9.refs_3_), channel_id=1, source_target_pairs={{0,1},{1,0},{2,3},{3,2},{4,5},{5,4},{6,7},{7,6},{8,9},{9,8},{10,11... | collective-permute-start | bytes 221192 | tf_op jit(solution)/shard_map/ppermute | solution.py:494
  29.9 1.3 %collective-permute-start.12 = (f32[144,128]{1,0:T(8,128)S(1)}, f32[144,128]{1,0:T(8,128)S(1)}, u32[]{:S(2)}, u32[]{:S(2)}) collective-permute-start(f32[144,128]{1,0:T(8,128)S(1)} %collective-permute-done.8.refs_2_), channel_id=1, source_target_pairs={{0,1},{1,0},{2,3},{3,2},{4,5},{5,4},{6,7},{7,6},{8,9},{9,8},{10,11... | collective-permute-start | bytes 221192 | tf_op jit(solution)/shard_map/ppermute | solution.py:494
  30.6 1.3 %collective-permute-start.11 = (f32[144,128]{1,0:T(8,128)S(1)}, f32[144,128]{1,0:T(8,128)S(1)}, u32[]{:S(2)}, u32[]{:S(2)}) collective-permute-start(f32[144,128]{1,0:T(8,128)S(1)} %collective-permute-done.7.refs_1_), channel_id=1, source_target_pairs={{0,1},{1,0},{2,3},{3,2},{4,5},{5,4},{6,7},{7,6},{8,9},{9,8},{10,11... | collective-permute-start | bytes 221192 | tf_op jit(solution)/shard_map/ppermute | solution.py:494

commit v2 on v1

--- a/solution.py
+++ b/solution.py
@@ -47,7 +47,7 @@
 
 def rsq(p):
     r = lax.rsqrt(p)
-    return r * (1.5 - (0.5 * p) * (r * r))
+    return r
 
 
 def lane(x, c):
@@ -257,8 +257,8 @@
     queue = []
     state = {}
 
-    def send(src, dst, n):
-        c = pltpu.make_async_copy(src, dst, sem.at[n])
+    def send(src, dst):
+        c = pltpu.make_async_copy(src, dst, sem.at[len(copies)])
         c.start()
         copies.append(c)
 
@@ -295,7 +295,7 @@
         z = six(linv, thirds(rk_ref[...]), NN)
         yield
         cf_ref[...] = six(linv, thirds(z), TN)
-        send(cf_ref, coef_out, 0)
+        send(cf_ref, coef_out)
         state["coef"] = True
 
     state["gram"] = {
@@ -326,15 +326,21 @@
             if not last:
                 y_ref[at, hi:] = src[at, hi:] - six(thirds(b), above, NN)
 
+        def ship_factor():
+            send(f_ref.at[lo:hi, :], fac_out.at[lo:hi, :])
+
+        def ship_basis(n):
+            at = slice(128 * n, min(128 * n + 128, n_rows))
+            send(y_ref.at[at, lo:hi], bas_out.at[at, lo:hi])
+
+        queue.append(ship_factor)
+        if last:
+            queue.append(functools.partial(residual, k))
         for n in range(-(-n_rows // 128)):
             queue.append(functools.partial(rows, n))
-        queue.append(functools.partial(residual, k))
-
-        def ship():
-            send(f_ref.at[lo:hi, :], fac_out.at[lo:hi, :], 1 + k)
-            send(y_ref.at[:, lo:hi], bas_out.at[:, lo:hi], 5 + k)
-
-        queue.append(ship)
+            queue.append(functools.partial(ship_basis, n))
+        if not last:
+            queue.append(functools.partial(residual, k))
 
     def residual(k):
         lo, hi = 128 * k, 128 * k + 128
@@ -357,7 +363,7 @@
     for f in queue:
         f()
     sq_ref[...] = jnp.sqrt(1.0 + state["sq"])
-    send(sq_ref, res_out, 9)
+    send(sq_ref, res_out)
     for c in copies:
         c.wait()
 
@@ -415,7 +421,7 @@
             pltpu.VMEM((1, 512), f32),
             pltpu.VMEM((2, 8, 64, 128), f32),
             pltpu.VMEM((2 * HALF, 128), f32),
-            pltpu.SemaphoreType.DMA((10,)),
+            pltpu.SemaphoreType.DMA((6 + 4 * -(-rows // 128),)),
         ],
         compiler_params=pltpu.CompilerParams(vmem_limit_bytes=32 << 20),
         name="factor_fit",

time: 50.7 us -> 49.5 us (0.976)
  Pallas kernels: 21.4 us -> 20.1 us
    pallas_call x1, Pallas kernels: 18.5 us -> 17.3 us  [fit_call(): pl.pallas_call(body, out_shape=(jax.ShapeDtypeStruct((512, 512), f32), ja...]
where the time goes in v2:
time: 49.5 us; the launch traced here: 49.3 us
  Pallas kernels  20.1 us (41%)
  waiting for transfers between devices  15.2 us (31%)
  starting transfers between devices  13 us (26%)
  between operations  0.84 us (2%)
    pallas_call x1, Pallas kernels, fit_call(): pl.pallas_call(body, out_shape=(jax.ShapeDtypeStruct((512, 512), f32), ja...  17.3 us
    ppermute x14, waiting for transfers between devices, swap(): return lax.ppermute(x, AXES, [(i, i ^ bit) for i in range(devices)])  15.2 us
    ppermute x14, starting transfers between devices, swap(): return lax.ppermute(x, AXES, [(i, i ^ bit) for i in range(devices)])  13 us
    pallas_call x1, Pallas kernels, gram_call(): pl.pallas_call(gram_kernel, out_shape=(half, half, jax.ShapeDtypeStruct(x...  2.81 us
  transfers between devices with their start and end apart: 14, of which 11 were waited for; matrix products, arithmetic and copies ran while one was open for 0% of the time, Pallas kernels for 0%

profile of v2, /device:TPU:0, one launch (start us, length us, event | category | flops | bytes accessed | tf_op | source)
XLA Modules:
  0.0 49.3 jit_solution(8027759254799258482)
XLA Ops:
  0.6 2.8 %gram.1 = (f32[576,128]{1,0:T(8,128)S(1)}, f32[576,128]{1,0:T(8,128)S(1)}, f32[512,512]{1,0:T(8,128)S(1)}) custom-call(f32[512,512]{1,0:T(8,128)} %x_hbm.1), custom_call_target="tpu_custom_call" | custom-call | tf_op jit(solution)/shard_map/gram/pallas_call | solution.py:471
  3.4 0.5 %collective-permute-start = (f32[576,128]{1,0:T(8,128)S(1)}, f32[576,128]{1,0:T(8,128)S(1)}, u32[]{:S(2)}, u32[]{:S(2)}) collective-permute-start(f32[576,128]{1,0:T(8,128)S(1)} %get-tuple-element.16), channel_id=1, source_target_pairs={{0,1},{1,0},{2,3},{3,2},{4,5},{5,4},{6,7},{7,6},{8,9},{9,8},{10,11... | collective-permute-start | bytes 884744 | tf_op jit(solution)/shard_map/ppermute | solution.py:500
  4.0 1.2 %collective-permute-done.got_ref = f32[576,128]{1,0:T(8,128)S(1)} collective-permute-done((f32[576,128]{1,0:T(8,128)S(1)}, f32[576,128]{1,0:T(8,128)S(1)}, u32[]{:S(2)}, u32[]{:S(2)}) %collective-permute-start) | collective-permute-done | bytes 294944 | tf_op jit(solution)/shard_map/ppermute | solution.py:500
  5.2 2.9 %collective-permute-start.1 = (f32[144,128]{1,0:T(8,128)S(1)}, f32[144,128]{1,0:T(8,128)S(1)}, u32[]{:S(2)}, u32[]{:S(2)}) collective-permute-start(f32[144,128]{1,0:T(8,128)S(1)} %get-tuple-element.18), channel_id=1, source_target_pairs={{0,2},{1,3},{2,0},{3,1},{4,6},{5,7},{6,4},{7,5},{8,10},{9,11},{10,... | collective-permute-start | bytes 221192 | tf_op jit(solution)/shard_map/ppermute | solution.py:500
  8.1 1.5 %collective-permute-start.2 = (f32[144,128]{1,0:T(8,128)S(1)}, f32[144,128]{1,0:T(8,128)S(1)}, u32[]{:S(2)}, u32[]{:S(2)}) collective-permute-start(f32[144,128]{1,0:T(8,128)S(1)} %get-tuple-element.19), channel_id=1, source_target_pairs={{0,4},{1,5},{2,6},{3,7},{4,0},{5,1},{6,2},{7,3},{8,12},{9,13},{10,... | collective-permute-start | bytes 221192 | tf_op jit(solution)/shard_map/ppermute | solution.py:500
  9.7 0.0 collective-permute-start.3
  9.7 1.0 %collective-permute-done.1 = f32[144,128]{1,0:T(8,128)S(1)} collective-permute-done((f32[144,128]{1,0:T(8,128)S(1)}, f32[144,128]{1,0:T(8,128)S(1)}, u32[]{:S(2)}, u32[]{:S(2)}) %collective-permute-start.1) | collective-permute-done | bytes 73760 | tf_op jit(solution)/shard_map/ppermute | solution.py:500
  10.7 1.8 %collective-permute-done.2 = f32[144,128]{1,0:T(8,128)S(1)} collective-permute-done((f32[144,128]{1,0:T(8,128)S(1)}, f32[144,128]{1,0:T(8,128)S(1)}, u32[]{:S(2)}, u32[]{:S(2)}) %collective-permute-start.2) | collective-permute-done | bytes 73760 | tf_op jit(solution)/shard_map/ppermute | solution.py:500
  12.5 2.4 %collective-permute-done.3 = f32[144,128]{1,0:T(8,128)S(1)} collective-permute-done((f32[144,128]{1,0:T(8,128)S(1)}, f32[144,128]{1,0:T(8,128)S(1)}, u32[]{:S(2)}, u32[]{:S(2)}) %collective-permute-start.3) | collective-permute-done | bytes 73760 | tf_op jit(solution)/shard_map/ppermute | solution.py:500
  14.9 3.7 %collective-permute-start.6 = (f32[144,128]{1,0:T(8,128)S(1)}, f32[144,128]{1,0:T(8,128)S(1)}, u32[]{:S(2)}, u32[]{:S(2)}) collective-permute-start(f32[144,128]{1,0:T(8,128)S(1)} %add_add_fusion.1), channel_id=1, source_target_pairs={{0,24},{1,25},{2,26},{3,27},{4,28},{5,29},{6,30},{7,31},{8,16},{9,... | collective-permute-start | bytes 221192 | tf_op jit(solution)/shard_map/ppermute | solution.py:500
  18.6 0.0 collective-permute-start.5
  18.6 0.8 %collective-permute-start.4 = (f32[144,128]{1,0:T(8,128)S(1)}, f32[144,128]{1,0:T(8,128)S(1)}, u32[]{:S(2)}, u32[]{:S(2)}) collective-permute-start(f32[144,128]{1,0:T(8,128)S(1)} %add_add_fusion.1), channel_id=1, source_target_pairs={{0,8},{1,9},{2,10},{3,11},{4,12},{5,13},{6,14},{7,15},{8,0},{9,1},... | collective-permute-start | bytes 221192 | tf_op jit(solution)/shard_map/ppermute | solution.py:500
  19.4 1.8 %collective-permute-done.6 = f32[144,128]{1,0:T(8,128)S(1)} collective-permute-done((f32[144,128]{1,0:T(8,128)S(1)}, f32[144,128]{1,0:T(8,128)S(1)}, u32[]{:S(2)}, u32[]{:S(2)}) %collective-permute-start.6) | collective-permute-done | bytes 73760 | tf_op jit(solution)/shard_map/ppermute | solution.py:500
  21.2 2.8 %collective-permute-done.5 = f32[144,128]{1,0:T(8,128)S(1)} collective-permute-done((f32[144,128]{1,0:T(8,128)S(1)}, f32[144,128]{1,0:T(8,128)S(1)}, u32[]{:S(2)}, u32[]{:S(2)}) %collective-permute-start.5) | collective-permute-done | bytes 73760 | tf_op jit(solution)/shard_map/ppermute | solution.py:500
  24.0 0.0 collective-permute-done.4
  24.0 0.0 copy-start
  24.0 0.8 %collective-permute-start.9 = (f32[144,128]{1,0:T(8,128)S(1)}, f32[144,128]{1,0:T(8,128)S(1)}, u32[]{:S(2)}, u32[]{:S(2)}) collective-permute-start(f32[144,128]{1,0:T(8,128)S(1)} %add_add_fusion.refs_0_), channel_id=1, source_target_pairs={{0,6},{1,7},{2,4},{3,5},{4,2},{5,3},{6,0},{7,1},{8,14},{9,15},{10,... | collective-permute-start | bytes 221192 | tf_op jit(solution)/shard_map/ppermute | solution.py:500
  24.8 1.5 %collective-permute-start.8 = (f32[144,128]{1,0:T(8,128)S(1)}, f32[144,128]{1,0:T(8,128)S(1)}, u32[]{:S(2)}, u32[]{:S(2)}) collective-permute-start(f32[144,128]{1,0:T(8,128)S(1)} %add_add_fusion.refs_0_), channel_id=1, source_target_pairs={{0,4},{1,5},{2,6},{3,7},{4,0},{5,1},{6,2},{7,3},{8,12},{9,13},{10,... | collective-permute-start | bytes 221192 | tf_op jit(solution)/shard_map/ppermute | solution.py:500
  26.3 1.3 %collective-permute-start.7 = (f32[144,128]{1,0:T(8,128)S(1)}, f32[144,128]{1,0:T(8,128)S(1)}, u32[]{:S(2)}, u32[]{:S(2)}) collective-permute-start(f32[144,128]{1,0:T(8,128)S(1)} %add_add_fusion.refs_0_), channel_id=1, source_target_pairs={{0,2},{1,3},{2,0},{3,1},{4,6},{5,7},{6,4},{7,5},{8,10},{9,11},{10,... | collective-permute-start | bytes 221192 | tf_op jit(solution)/shard_map/ppermute | solution.py:500
  27.6 0.0 collective-permute-start.10
  27.6 1.9 %collective-permute-done.9.refs_3_ = f32[144,128]{1,0:T(8,128)S(1)} collective-permute-done((f32[144,128]{1,0:T(8,128)S(1)}, f32[144,128]{1,0:T(8,128)S(1)}, u32[]{:S(2)}, u32[]{:S(2)}) %collective-permute-start.9) | collective-permute-done | bytes 73760 | tf_op jit(solution)/shard_map/ppermute | solution.py:500
  29.4 0.0 collective-permute-start.13
  29.4 0.5 %collective-permute-done.8.refs_2_ = f32[144,128]{1,0:T(8,128)S(1)} collective-permute-done((f32[144,128]{1,0:T(8,128)S(1)}, f32[144,128]{1,0:T(8,128)S(1)}, u32[]{:S(2)}, u32[]{:S(2)}) %collective-permute-start.8) | collective-permute-done | bytes 73760 | tf_op jit(solution)/shard_map/ppermute | solution.py:500
  29.9 0.0 collective-permute-start.12
  29.9 0.7 %collective-permute-done.7.refs_1_ = f32[144,128]{1,0:T(8,128)S(1)} collective-permute-done((f32[144,128]{1,0:T(8,128)S(1)}, f32[144,128]{1,0:T(8,128)S(1)}, u32[]{:S(2)}, u32[]{:S(2)}) %collective-permute-start.7) | collective-permute-done | bytes 73760 | tf_op jit(solution)/shard_map/ppermute | solution.py:500
  30.6 0.0 collective-permute-start.11
  30.6 0.0 copy-done
  30.6 0.1 copy.6.refs_9_
  30.7 0.0 collective-permute-done.10.refs_4_
  30.7 0.0 collective-permute-done.13.refs_7_
  30.7 0.5 collective-permute-done.12.refs_6_
  31.2 0.7 %collective-permute-done.11.refs_5_ = f32[144,128]{1,0:T(8,128)S(1)} collective-permute-done((f32[144,128]{1,0:T(8,128)S(1)}, f32[144,128]{1,0:T(8,128)S(1)}, u32[]{:S(2)}, u32[]{:S(2)}) %collective-permute-start.11) | collective-permute-done | bytes 73760 | tf_op jit(solution)/shard_map/ppermute | solution.py:500
  31.9 17.3 %factor_fit.1 = (f32[512,512]{1,0:T(8,128)}, f32[64,512]{1,0:T(8,128)}, f32[512,512]{1,0:T(8,128)}, f32[1,512]{1,0:T(1,128)}) custom-call(f32[144,128]{1,0:T(8,128)S(1)} %add_add_fusion.refs_0_, f32[144,128]{1,0:T(8,128)S(1)} %collective-permute-done.7.refs_1_, f32[144,128]{1,0:T(8,128)S(1)} %collective-permute-done.8.refs_2_, ...), custom_call_target="tpu_custom_call" | custom-call | tf_op jit(solution)/shard_map/factor_fit/pallas_call | solution.py:402
  (3 shorter events, 0.1 us)
Async XLA Ops:
  3.4 1.7 %collective-permute-start = (f32[576,128]{1,0:T(8,128)S(1)}, f32[576,128]{1,0:T(8,128)S(1)}, u32[]{:S(2)}, u32[]{:S(2)}) collective-permute-start(f32[576,128]{1,0:T(8,128)S(1)} %get-tuple-element.16), channel_id=1, source_target_pairs={{0,1},{1,0},{2,3},{3,2},{4,5},{5,4},{6,7},{7,6},{8,9},{9,8},{10,11... | collective-permute-start | bytes 884744 | tf_op jit(solution)/shard_map/ppermute | solution.py:500
  5.2 5.5 %collective-permute-start.1 = (f32[144,128]{1,0:T(8,128)S(1)}, f32[144,128]{1,0:T(8,128)S(1)}, u32[]{:S(2)}, u32[]{:S(2)}) collective-permute-start(f32[144,128]{1,0:T(8,128)S(1)} %get-tuple-element.18), channel_id=1, source_target_pairs={{0,2},{1,3},{2,0},{3,1},{4,6},{5,7},{6,4},{7,5},{8,10},{9,11},{10,... | collective-permute-start | bytes 221192 | tf_op jit(solution)/shard_map/ppermute | solution.py:500
  8.1 4.4 %collective-permute-start.2 = (f32[144,128]{1,0:T(8,128)S(1)}, f32[144,128]{1,0:T(8,128)S(1)}, u32[]{:S(2)}, u32[]{:S(2)}) collective-permute-start(f32[144,128]{1,0:T(8,128)S(1)} %get-tuple-element.19), channel_id=1, source_target_pairs={{0,4},{1,5},{2,6},{3,7},{4,0},{5,1},{6,2},{7,3},{8,12},{9,13},{10,... | collective-permute-start | bytes 221192 | tf_op jit(solution)/shard_map/ppermute | solution.py:500
  9.7 5.3 %collective-permute-start.3 = (f32[144,128]{1,0:T(8,128)S(1)}, f32[144,128]{1,0:T(8,128)S(1)}, u32[]{:S(2)}, u32[]{:S(2)}) collective-permute-start(f32[144,128]{1,0:T(8,128)S(1)} %get-tuple-element.20), channel_id=1, source_target_pairs={{0,6},{1,7},{2,4},{3,5},{4,2},{5,3},{6,0},{7,1},{8,14},{9,15},{10,... | collective-permute-start | bytes 221192 | tf_op jit(solution)/shard_map/ppermute | solution.py:500
  14.9 6.2 %collective-permute-start.6 = (f32[144,128]{1,0:T(8,128)S(1)}, f32[144,128]{1,0:T(8,128)S(1)}, u32[]{:S(2)}, u32[]{:S(2)}) collective-permute-start(f32[144,128]{1,0:T(8,128)S(1)} %add_add_fusion.1), channel_id=1, source_target_pairs={{0,24},{1,25},{2,26},{3,27},{4,28},{5,29},{6,30},{7,31},{8,16},{9,... | collective-permute-start | bytes 221192 | tf_op jit(solution)/shard_map/ppermute | solution.py:500
  18.6 5.4 %collective-permute-start.5 = (f32[144,128]{1,0:T(8,128)S(1)}, f32[144,128]{1,0:T(8,128)S(1)}, u32[]{:S(2)}, u32[]{:S(2)}) collective-permute-start(f32[144,128]{1,0:T(8,128)S(1)} %add_add_fusion.1), channel_id=1, source_target_pairs={{0,16},{1,17},{2,18},{3,19},{4,20},{5,21},{6,22},{7,23},{8,24},{9,... | collective-permute-start | bytes 221192 | tf_op jit(solution)/shard_map/ppermute | solution.py:500
  18.6 5.4 %collective-permute-start.4 = (f32[144,128]{1,0:T(8,128)S(1)}, f32[144,128]{1,0:T(8,128)S(1)}, u32[]{:S(2)}, u32[]{:S(2)}) collective-permute-start(f32[144,128]{1,0:T(8,128)S(1)} %add_add_fusion.1), channel_id=1, source_target_pairs={{0,8},{1,9},{2,10},{3,11},{4,12},{5,13},{6,14},{7,15},{8,0},{9,1},... | collective-permute-start | bytes 221192 | tf_op jit(solution)/shard_map/ppermute | solution.py:500
  24.0 6.6 %copy-start = (s32[64]{0:T(128)S(1)}, s32[64]{0:T(128)}, u32[]{:S(2)}) copy-start(s32[64]{0:T(128)} %param.3) | copy-start | bytes 772
  24.0 5.4 %collective-permute-start.9 = (f32[144,128]{1,0:T(8,128)S(1)}, f32[144,128]{1,0:T(8,128)S(1)}, u32[]{:S(2)}, u32[]{:S(2)}) collective-permute-start(f32[144,128]{1,0:T(8,128)S(1)} %add_add_fusion.refs_0_), channel_id=1, source_target_pairs={{0,6},{1,7},{2,4},{3,5},{4,2},{5,3},{6,0},{7,1},{8,14},{9,15},{10,... | collective-permute-start | bytes 221192 | tf_op jit(solution)/shard_map/ppermute | solution.py:500
  24.8 5.1 %collective-permute-start.8 = (f32[144,128]{1,0:T(8,128)S(1)}, f32[144,128]{1,0:T(8,128)S(1)}, u32[]{:S(2)}, u32[]{:S(2)}) collective-permute-start(f32[144,128]{1,0:T(8,128)S(1)} %add_add_fusion.refs_0_), channel_id=1, source_target_pairs={{0,4},{1,5},{2,6},{3,7},{4,0},{5,1},{6,2},{7,3},{8,12},{9,13},{10,... | collective-permute-start | bytes 221192 | tf_op jit(solution)/shard_map/ppermute | solution.py:500
  26.3 4.4 %collective-permute-start.7 = (f32[144,128]{1,0:T(8,128)S(1)}, f32[144,128]{1,0:T(8,128)S(1)}, u32[]{:S(2)}, u32[]{:S(2)}) collective-permute-start(f32[144,128]{1,0:T(8,128)S(1)} %add_add_fusion.refs_0_), channel_id=1, source_target_pairs={{0,2},{1,3},{2,0},{3,1},{4,6},{5,7},{6,4},{7,5},{8,10},{9,11},{10,... | collective-permute-start | bytes 221192 | tf_op jit(solution)/shard_map/ppermute | solution.py:500
  27.6 3.1 %collective-permute-start.10 = (f32[144,128]{1,0:T(8,128)S(1)}, f32[144,128]{1,0:T(8,128)S(1)}, u32[]{:S(2)}, u32[]{:S(2)}) collective-permute-start(f32[144,128]{1,0:T(8,128)S(1)} %add_add_fusion.refs_0_), channel_id=1, source_target_pairs={{0,1},{1,0},{2,3},{3,2},{4,5},{5,4},{6,7},{7,6},{8,9},{9,8},{10,11... | collective-permute-start | bytes 221192 | tf_op jit(solution)/shard_map/ppermute | solution.py:500
  29.4 1.3 %collective-permute-start.13 = (f32[144,128]{1,0:T(8,128)S(1)}, f32[144,128]{1,0:T(8,128)S(1)}, u32[]{:S(2)}, u32[]{:S(2)}) collective-permute-start(f32[144,128]{1,0:T(8,128)S(1)} %collective-permute-done.9.refs_3_), channel_id=1, source_target_pairs={{0,1},{1,0},{2,3},{3,2},{4,5},{5,4},{6,7},{7,6},{8,9},{9,8},{10,11... | collective-permute-start | bytes 221192 | tf_op jit(solution)/shard_map/ppermute | solution.py:500
  29.9 1.3 %collective-permute-start.12 = (f32[144,128]{1,0:T(8,128)S(1)}, f32[144,128]{1,0:T(8,128)S(1)}, u32[]{:S(2)}, u32[]{:S(2)}) collective-permute-start(f32[144,128]{1,0:T(8,128)S(1)} %collective-permute-done.8.refs_2_), channel_id=1, source_target_pairs={{0,1},{1,0},{2,3},{3,2},{4,5},{5,4},{6,7},{7,6},{8,9},{9,8},{10,11... | collective-permute-start | bytes 221192 | tf_op jit(solution)/shard_map/ppermute | solution.py:500
  30.6 1.3 %collective-permute-start.11 = (f32[144,128]{1,0:T(8,128)S(1)}, f32[144,128]{1,0:T(8,128)S(1)}, u32[]{:S(2)}, u32[]{:S(2)}) collective-permute-start(f32[144,128]{1,0:T(8,128)S(1)} %collective-permute-done.7.refs_1_), channel_id=1, source_target_pairs={{0,1},{1,0},{2,3},{3,2},{4,5},{5,4},{6,7},{7,6},{8,9},{9,8},{10,11... | collective-permute-start | bytes 221192 | tf_op jit(solution)/shard_map/ppermute | solution.py:500

commit v3 on v2

--- a/solution.py
+++ b/solution.py
@@ -375,19 +375,16 @@
         at = (core ^ (m // 4)) * HALF + (q ^ (m % 4)) * PIECE
         g_ref[pl.ds(pl.multiple_of(at, PIECE), PIECE), :] = pieces[m][...] / total
     n = 0
-    for i in range(4):
-        rows = slice(128 * i, 128 * i + 64)
-        t_ref[rows, 128 * i : 128 * i + 128] = g_ref[64 * n : 64 * n + 64, :]
-        n += 1
-        for j in range(i + 1, 4):
-            t_ref[128 * i : 128 * i + 128, 128 * j : 128 * j + 128] = g_ref[64 * n : 64 * n + 128, :]
-            n += 2
-    for i in range(4):
-        x = g_ref[64 * (n + i // 2) : 64 * (n + i // 2) + 64, :]
-        if i % 2 == 0:
-            x = pltpu.roll(x, 64, 1)
-        t_ref[128 * i + 64 : 128 * i + 128, 128 * i : 128 * i + 128] = x
-
+    for i, first, stop in ((0, 0, 4), (1, 1, 2), (0, 0, 0), (1, 2, 4), (2, 2, 4), (3, 3, 4), (2, 2, 2)):
+        for j in range(first, stop):
+            tall = 64 if i == j else 128
+            t_ref[128 * i : 128 * i + tall, 128 * j : 128 * j + 128] = g_ref[64 * n : 64 * n + tall, :]
+            n += tall // 64
+        if first == stop:
+            x = g_ref[64 * n : 64 * n + 64, :]
+            t_ref[128 * i + 64 : 128 * i + 128, 128 * i : 128 * i + 128] = pltpu.roll(x, 64, 1)
+            t_ref[128 * i + 192 : 128 * i + 256, 128 * i + 128 : 128 * i + 256] = x
+            n += 1
 
 def fit_call(pieces, data, anchors, total):
     f32 = jnp.float32
@@ -432,7 +429,29 @@
     return lax.axis_index("wide") * lax.axis_size("narrow") + lax.axis_index("narrow")
 
 
-def gram_kernel(x_hbm, own_ref, other_ref, x_ref, both_ref, sem):
+def gram_half(x, half, out_ref):
+    n = 0
+
+    def put(unit):
+        nonlocal n
+        out_ref[64 * n : 64 * n + 64, :] = unit
+        n += 1
+
+    corners = []
+    for i, first, stop in ((0, 0, 4), (1, 1, 2)) if half == 0 else ((1, 2, 4), (2, 2, 4), (3, 3, 4)):
+        row = mm(x[:, 128 * i : 128 * i + 128], x[:, 128 * first : 128 * stop], TN)
+        for j in range(first, stop):
+            block = row[:, 128 * (j - first) : 128 * (j - first) + 128]
+            put(block[:64])
+            if i == j:
+                corners.append(block[64:])
+            else:
+                put(block[64:])
+    lanes = lax.broadcasted_iota(jnp.int32, (64, 128), 1)
+    put(jnp.where(lanes < 64, pltpu.roll(corners[0], 64, 1), corners[1]))
+
+
+def first_kernel(x_hbm, out_ref, x_ref, sem):
     rows = x_ref.shape[0] // 4
     copies = []
     for c in range(4):
@@ -441,42 +460,39 @@
         copies[-1].start()
     for c in copies:
         c.wait()
-    x = x_ref[...]
-
-    def put(n, unit):
-        both_ref[n // 9, 64 * (n % 9) : 64 * (n % 9) + 64, :] = unit
-
-    n = 0
-    corners = []
-    for i in range(4):
-        row = mm(x[:, 128 * i : 128 * i + 128], x[:, 128 * i :], TN)
-        for j in range(4 - i):
-            put(n, row[:64, 128 * j : 128 * j + 128])
-            n += 1
-            if j:
-                put(n, row[64:, 128 * j : 128 * j + 128])
-                n += 1
-        corners.append(row[64:, :128])
-    lanes = lax.broadcasted_iota(jnp.int32, (64, 128), 1)
-    for i in (0, 2):
-        put(n, jnp.where(lanes < 64, pltpu.roll(corners[i], 64, 1), corners[i + 1]))
-        n += 1
     bit = lax.rem(my_index(), 2)
-    own_ref[...] = both_ref[bit]
-    other_ref[...] = both_ref[1 - bit]
-
-
-def gram_call(x):
+    for half in (0, 1):
+        pl.when(bit != half)(lambda half=half: gram_half(x_ref[...], half, out_ref))
+
+
+def second_kernel(x_ref, out_ref):
+    bit = lax.rem(my_index(), 2)
+    for half in (0, 1):
+        pl.when(bit == half)(lambda half=half: gram_half(x_ref[...], half, out_ref))
+
+
+def gram_calls(x):
     half = jax.ShapeDtypeStruct((HALF, 128), jnp.float32)
-    return pl.pallas_call(
-        gram_kernel,
-        out_shape=(half, half, jax.ShapeDtypeStruct(x.shape, x.dtype)),
+    vmem = pl.BlockSpec(memory_space=pltpu.VMEM)
+    cost = pl.CostEstimate(flops=6 * 2 * x.shape[0] * 128 * 640, bytes_accessed=2 << 20, transcendentals=0)
+    other, kept = pl.pallas_call(
+        first_kernel,
+        out_shape=(half, jax.ShapeDtypeStruct(x.shape, x.dtype)),
         in_specs=[pl.BlockSpec(memory_space=pltpu.HBM)],
-        out_specs=(pl.BlockSpec(memory_space=pltpu.VMEM),) * 3,
-        scratch_shapes=[pltpu.VMEM((2, HALF, 128), jnp.float32), pltpu.SemaphoreType.DMA((4,))],
+        out_specs=(vmem, vmem),
+        scratch_shapes=[pltpu.SemaphoreType.DMA((4,))],
         compiler_params=pltpu.CompilerParams(vmem_limit_bytes=16 << 20),
-        name="gram",
+        cost_estimate=cost,
+        name="gram_other",
     )(pltpu.with_memory_space_constraint(x, pltpu.HBM))
+    own = pl.pallas_call(
+        second_kernel,
+        out_shape=half,
+        compiler_params=pltpu.CompilerParams(vmem_limit_bytes=16 << 20),
+        cost_estimate=cost,
+        name="gram_own",
+    )(kept)
+    return own, other, kept
 
 
 def split_kernel(own_ref, got_ref, *outs):
@@ -501,7 +517,7 @@
 
 
 def total_gram(x, devices):
-    own, other, kept = gram_call(x)
+    own, other, kept = gram_calls(x)
     parts = split_call(own, swap(other, 1, devices))
     got = [swap(parts[m], 2 * m, devices) for m in (1, 2, 3)]
     piece = (parts[0] + got[0]) + (got[1] + got[2])

time: 49.5 us -> 48.8 us (0.986)
  waiting for transfers between devices: 15.2 us -> 14.2 us
    ppermute x14, waiting for transfers between devices: 15.2 us -> 14.2 us  [swap(): return lax.ppermute(x, AXES, [(i, i ^ bit) for i in range(devices)])]
    pallas_call x1 -> x2, Pallas kernels: 2.81 us -> 3.05 us  [the longest x1 2.05 us: gram_calls(): pl.pallas_call(first_kernel, out_shape=(half, jax.ShapeDtypeStruct(x.shap...]
  transfers between devices with their start and end apart: 14 -> 14, of which waited for: 11 -> 11; matrix products, arithmetic and copies ran while one was open for 0% -> 0% of each run, Pallas kernels for 0% -> 2%
where the time goes in v3:
time: 48.8 us; the launch traced here: 48.6 us
  Pallas kernels  20.4 us (42%)
  waiting for transfers between devices  14.2 us (29%)
  starting transfers between devices  13 us (27%)
  between operations  0.86 us (2%)
    pallas_call x1, Pallas kernels, fit_call(): pl.pallas_call(body, out_shape=(jax.ShapeDtypeStruct((512, 512), f32), ja...  17.4 us
    ppermute x14, waiting for transfers between devices, swap(): return lax.ppermute(x, AXES, [(i, i ^ bit) for i in range(devices)])  14.2 us
    ppermute x14, starting transfers between devices, swap(): return lax.ppermute(x, AXES, [(i, i ^ bit) for i in range(devices)])  13 us
    pallas_call x1, Pallas kernels, gram_calls(): pl.pallas_call(first_kernel, out_shape=(half, jax.ShapeDtypeStruct(x.shap...  2.05 us
    pallas_call x1, Pallas kernels, gram_calls(): pl.pallas_call(second_kernel, out_shape=half, compiler_params=pltpu.Compi...  1 us
  transfers between devices with their start and end apart: 14, of which 11 were waited for; matrix products, arithmetic and copies ran while one was open for 0% of the time, Pallas kernels for 2%

profile of v3, /device:TPU:0, one launch (start us, length us, event | category | flops | bytes accessed | tf_op | source)
XLA Modules:
  0.0 48.6 jit_solution(11786562523781989013)
XLA Ops:
  0.6 2.0 %gram_other.1 = (f32[576,128]{1,0:T(8,128)S(1)}, f32[512,512]{1,0:T(8,128)S(1)}) custom-call(f32[512,512]{1,0:T(8,128)} %x_hbm.1), custom_call_target="tpu_custom_call" | custom-call | flops 503316480 | bytes 2097152 | tf_op jit(solution)/shard_map/gram_other/pallas_call | solution.py:478
  2.7 0.5 %collective-permute-start = (f32[576,128]{1,0:T(8,128)S(1)}, f32[576,128]{1,0:T(8,128)S(1)}, u32[]{:S(2)}, u32[]{:S(2)}) collective-permute-start(f32[576,128]{1,0:T(8,128)S(1)} %get-tuple-element.15), channel_id=1, source_target_pairs={{0,1},{1,0},{2,3},{3,2},{4,5},{5,4},{6,7},{7,6},{8,9},{9,8},{10,11... | collective-permute-start | bytes 884744 | tf_op jit(solution)/shard_map/ppermute | solution.py:516
  3.2 1.0 %gram_own.1.own_ref = f32[576,128]{1,0:T(8,128)S(1)} custom-call(f32[512,512]{1,0:T(8,128)S(1)} %get-tuple-element.14.x_ref.refs_8_), custom_call_target="tpu_custom_call" | custom-call | flops 503316480 | bytes 2097152 | tf_op jit(solution)/shard_map/gram_own/pallas_call | solution.py:488
  4.2 0.2 collective-permute-done.got_ref
  4.4 2.9 %collective-permute-start.1 = (f32[144,128]{1,0:T(8,128)S(1)}, f32[144,128]{1,0:T(8,128)S(1)}, u32[]{:S(2)}, u32[]{:S(2)}) collective-permute-start(f32[144,128]{1,0:T(8,128)S(1)} %get-tuple-element.17), channel_id=1, source_target_pairs={{0,2},{1,3},{2,0},{3,1},{4,6},{5,7},{6,4},{7,5},{8,10},{9,11},{10,... | collective-permute-start | bytes 221192 | tf_op jit(solution)/shard_map/ppermute | solution.py:516
  7.4 1.5 %collective-permute-start.2 = (f32[144,128]{1,0:T(8,128)S(1)}, f32[144,128]{1,0:T(8,128)S(1)}, u32[]{:S(2)}, u32[]{:S(2)}) collective-permute-start(f32[144,128]{1,0:T(8,128)S(1)} %get-tuple-element.18), channel_id=1, source_target_pairs={{0,4},{1,5},{2,6},{3,7},{4,0},{5,1},{6,2},{7,3},{8,12},{9,13},{10,... | collective-permute-start | bytes 221192 | tf_op jit(solution)/shard_map/ppermute | solution.py:516
  8.9 0.0 collective-permute-start.3
  8.9 1.0 %collective-permute-done.1 = f32[144,128]{1,0:T(8,128)S(1)} collective-permute-done((f32[144,128]{1,0:T(8,128)S(1)}, f32[144,128]{1,0:T(8,128)S(1)}, u32[]{:S(2)}, u32[]{:S(2)}) %collective-permute-start.1) | collective-permute-done | bytes 73760 | tf_op jit(solution)/shard_map/ppermute | solution.py:516
  9.9 1.8 %collective-permute-done.2 = f32[144,128]{1,0:T(8,128)S(1)} collective-permute-done((f32[144,128]{1,0:T(8,128)S(1)}, f32[144,128]{1,0:T(8,128)S(1)}, u32[]{:S(2)}, u32[]{:S(2)}) %collective-permute-start.2) | collective-permute-done | bytes 73760 | tf_op jit(solution)/shard_map/ppermute | solution.py:516
  11.7 2.4 %collective-permute-done.3 = f32[144,128]{1,0:T(8,128)S(1)} collective-permute-done((f32[144,128]{1,0:T(8,128)S(1)}, f32[144,128]{1,0:T(8,128)S(1)}, u32[]{:S(2)}, u32[]{:S(2)}) %collective-permute-start.3) | collective-permute-done | bytes 73760 | tf_op jit(solution)/shard_map/ppermute | solution.py:516
  14.2 3.7 %collective-permute-start.6 = (f32[144,128]{1,0:T(8,128)S(1)}, f32[144,128]{1,0:T(8,128)S(1)}, u32[]{:S(2)}, u32[]{:S(2)}) collective-permute-start(f32[144,128]{1,0:T(8,128)S(1)} %add_add_fusion.1), channel_id=1, source_target_pairs={{0,24},{1,25},{2,26},{3,27},{4,28},{5,29},{6,30},{7,31},{8,16},{9,... | collective-permute-start | bytes 221192 | tf_op jit(solution)/shard_map/ppermute | solution.py:516
  17.8 0.0 collective-permute-start.5
  17.8 0.8 %collective-permute-start.4 = (f32[144,128]{1,0:T(8,128)S(1)}, f32[144,128]{1,0:T(8,128)S(1)}, u32[]{:S(2)}, u32[]{:S(2)}) collective-permute-start(f32[144,128]{1,0:T(8,128)S(1)} %add_add_fusion.1), channel_id=1, source_target_pairs={{0,8},{1,9},{2,10},{3,11},{4,12},{5,13},{6,14},{7,15},{8,0},{9,1},... | collective-permute-start | bytes 221192 | tf_op jit(solution)/shard_map/ppermute | solution.py:516
  18.6 1.8 %collective-permute-done.6 = f32[144,128]{1,0:T(8,128)S(1)} collective-permute-done((f32[144,128]{1,0:T(8,128)S(1)}, f32[144,128]{1,0:T(8,128)S(1)}, u32[]{:S(2)}, u32[]{:S(2)}) %collective-permute-start.6) | collective-permute-done | bytes 73760 | tf_op jit(solution)/shard_map/ppermute | solution.py:516
  20.4 2.8 %collective-permute-done.5 = f32[144,128]{1,0:T(8,128)S(1)} collective-permute-done((f32[144,128]{1,0:T(8,128)S(1)}, f32[144,128]{1,0:T(8,128)S(1)}, u32[]{:S(2)}, u32[]{:S(2)}) %collective-permute-start.5) | collective-permute-done | bytes 73760 | tf_op jit(solution)/shard_map/ppermute | solution.py:516
  23.2 0.0 collective-permute-done.4
  23.2 0.0 copy-start
  23.2 0.8 %collective-permute-start.9 = (f32[144,128]{1,0:T(8,128)S(1)}, f32[144,128]{1,0:T(8,128)S(1)}, u32[]{:S(2)}, u32[]{:S(2)}) collective-permute-start(f32[144,128]{1,0:T(8,128)S(1)} %add_add_fusion.refs_0_), channel_id=1, source_target_pairs={{0,6},{1,7},{2,4},{3,5},{4,2},{5,3},{6,0},{7,1},{8,14},{9,15},{10,... | collective-permute-start | bytes 221192 | tf_op jit(solution)/shard_map/ppermute | solution.py:516
  24.0 1.5 %collective-permute-start.8 = (f32[144,128]{1,0:T(8,128)S(1)}, f32[144,128]{1,0:T(8,128)S(1)}, u32[]{:S(2)}, u32[]{:S(2)}) collective-permute-start(f32[144,128]{1,0:T(8,128)S(1)} %add_add_fusion.refs_0_), channel_id=1, source_target_pairs={{0,4},{1,5},{2,6},{3,7},{4,0},{5,1},{6,2},{7,3},{8,12},{9,13},{10,... | collective-permute-start | bytes 221192 | tf_op jit(solution)/shard_map/ppermute | solution.py:516
  25.5 1.3 %collective-permute-start.7 = (f32[144,128]{1,0:T(8,128)S(1)}, f32[144,128]{1,0:T(8,128)S(1)}, u32[]{:S(2)}, u32[]{:S(2)}) collective-permute-start(f32[144,128]{1,0:T(8,128)S(1)} %add_add_fusion.refs_0_), channel_id=1, source_target_pairs={{0,2},{1,3},{2,0},{3,1},{4,6},{5,7},{6,4},{7,5},{8,10},{9,11},{10,... | collective-permute-start | bytes 221192 | tf_op jit(solution)/shard_map/ppermute | solution.py:516
  26.8 0.0 collective-permute-start.10
  26.8 1.9 %collective-permute-done.9.refs_3_ = f32[144,128]{1,0:T(8,128)S(1)} collective-permute-done((f32[144,128]{1,0:T(8,128)S(1)}, f32[144,128]{1,0:T(8,128)S(1)}, u32[]{:S(2)}, u32[]{:S(2)}) %collective-permute-start.9) | collective-permute-done | bytes 73760 | tf_op jit(solution)/shard_map/ppermute | solution.py:516
  28.7 0.0 collective-permute-start.13
  28.7 0.5 %collective-permute-done.8.refs_2_ = f32[144,128]{1,0:T(8,128)S(1)} collective-permute-done((f32[144,128]{1,0:T(8,128)S(1)}, f32[144,128]{1,0:T(8,128)S(1)}, u32[]{:S(2)}, u32[]{:S(2)}) %collective-permute-start.8) | collective-permute-done | bytes 73760 | tf_op jit(solution)/shard_map/ppermute | solution.py:516
  29.2 0.0 collective-permute-start.12
  29.2 0.7 %collective-permute-done.7.refs_1_ = f32[144,128]{1,0:T(8,128)S(1)} collective-permute-done((f32[144,128]{1,0:T(8,128)S(1)}, f32[144,128]{1,0:T(8,128)S(1)}, u32[]{:S(2)}, u32[]{:S(2)}) %collective-permute-start.7) | collective-permute-done | bytes 73760 | tf_op jit(solution)/shard_map/ppermute | solution.py:516
  29.8 0.0 collective-permute-start.11
  29.8 0.0 copy-done
  29.8 0.1 copy.6.refs_9_
  29.9 0.0 collective-permute-done.10.refs_4_
  29.9 0.0 collective-permute-done.13.refs_7_
  30.0 0.5 collective-permute-done.12.refs_6_
  30.4 0.7 %collective-permute-done.11.refs_5_ = f32[144,128]{1,0:T(8,128)S(1)} collective-permute-done((f32[144,128]{1,0:T(8,128)S(1)}, f32[144,128]{1,0:T(8,128)S(1)}, u32[]{:S(2)}, u32[]{:S(2)}) %collective-permute-start.11) | collective-permute-done | bytes 73760 | tf_op jit(solution)/shard_map/ppermute | solution.py:516
  31.1 17.4 %factor_fit.1 = (f32[512,512]{1,0:T(8,128)}, f32[64,512]{1,0:T(8,128)}, f32[512,512]{1,0:T(8,128)}, f32[1,512]{1,0:T(1,128)}) custom-call(f32[144,128]{1,0:T(8,128)S(1)} %add_add_fusion.refs_0_, f32[144,128]{1,0:T(8,128)S(1)} %collective-permute-done.7.refs_1_, f32[144,128]{1,0:T(8,128)S(1)} %collective-permute-done.8.refs_2_, ...), custom_call_target="tpu_custom_call" | custom-call | tf_op jit(solution)/shard_map/factor_fit/pallas_call | solution.py:399
  (3 shorter events, 0.1 us)
Async XLA Ops:
  2.7 1.7 %collective-permute-start = (f32[576,128]{1,0:T(8,128)S(1)}, f32[576,128]{1,0:T(8,128)S(1)}, u32[]{:S(2)}, u32[]{:S(2)}) collective-permute-start(f32[576,128]{1,0:T(8,128)S(1)} %get-tuple-element.15), channel_id=1, source_target_pairs={{0,1},{1,0},{2,3},{3,2},{4,5},{5,4},{6,7},{7,6},{8,9},{9,8},{10,11... | collective-permute-start | bytes 884744 | tf_op jit(solution)/shard_map/ppermute | solution.py:516
  4.4 5.5 %collective-permute-start.1 = (f32[144,128]{1,0:T(8,128)S(1)}, f32[144,128]{1,0:T(8,128)S(1)}, u32[]{:S(2)}, u32[]{:S(2)}) collective-permute-start(f32[144,128]{1,0:T(8,128)S(1)} %get-tuple-element.17), channel_id=1, source_target_pairs={{0,2},{1,3},{2,0},{3,1},{4,6},{5,7},{6,4},{7,5},{8,10},{9,11},{10,... | collective-permute-start | bytes 221192 | tf_op jit(solution)/shard_map/ppermute | solution.py:516
  7.4 4.4 %collective-permute-start.2 = (f32[144,128]{1,0:T(8,128)S(1)}, f32[144,128]{1,0:T(8,128)S(1)}, u32[]{:S(2)}, u32[]{:S(2)}) collective-permute-start(f32[144,128]{1,0:T(8,128)S(1)} %get-tuple-element.18), channel_id=1, source_target_pairs={{0,4},{1,5},{2,6},{3,7},{4,0},{5,1},{6,2},{7,3},{8,12},{9,13},{10,... | collective-permute-start | bytes 221192 | tf_op jit(solution)/shard_map/ppermute | solution.py:516
  8.9 5.3 %collective-permute-start.3 = (f32[144,128]{1,0:T(8,128)S(1)}, f32[144,128]{1,0:T(8,128)S(1)}, u32[]{:S(2)}, u32[]{:S(2)}) collective-permute-start(f32[144,128]{1,0:T(8,128)S(1)} %get-tuple-element.19), channel_id=1, source_target_pairs={{0,6},{1,7},{2,4},{3,5},{4,2},{5,3},{6,0},{7,1},{8,14},{9,15},{10,... | collective-permute-start | bytes 221192 | tf_op jit(solution)/shard_map/ppermute | solution.py:516
  14.2 6.2 %collective-permute-start.6 = (f32[144,128]{1,0:T(8,128)S(1)}, f32[144,128]{1,0:T(8,128)S(1)}, u32[]{:S(2)}, u32[]{:S(2)}) collective-permute-start(f32[144,128]{1,0:T(8,128)S(1)} %add_add_fusion.1), channel_id=1, source_target_pairs={{0,24},{1,25},{2,26},{3,27},{4,28},{5,29},{6,30},{7,31},{8,16},{9,... | collective-permute-start | bytes 221192 | tf_op jit(solution)/shard_map/ppermute | solution.py:516
  17.8 5.4 %collective-permute-start.5 = (f32[144,128]{1,0:T(8,128)S(1)}, f32[144,128]{1,0:T(8,128)S(1)}, u32[]{:S(2)}, u32[]{:S(2)}) collective-permute-start(f32[144,128]{1,0:T(8,128)S(1)} %add_add_fusion.1), channel_id=1, source_target_pairs={{0,16},{1,17},{2,18},{3,19},{4,20},{5,21},{6,22},{7,23},{8,24},{9,... | collective-permute-start | bytes 221192 | tf_op jit(solution)/shard_map/ppermute | solution.py:516
  17.8 5.4 %collective-permute-start.4 = (f32[144,128]{1,0:T(8,128)S(1)}, f32[144,128]{1,0:T(8,128)S(1)}, u32[]{:S(2)}, u32[]{:S(2)}) collective-permute-start(f32[144,128]{1,0:T(8,128)S(1)} %add_add_fusion.1), channel_id=1, source_target_pairs={{0,8},{1,9},{2,10},{3,11},{4,12},{5,13},{6,14},{7,15},{8,0},{9,1},... | collective-permute-start | bytes 221192 | tf_op jit(solution)/shard_map/ppermute | solution.py:516
  23.2 6.6 %copy-start = (s32[64]{0:T(128)S(1)}, s32[64]{0:T(128)}, u32[]{:S(2)}) copy-start(s32[64]{0:T(128)} %param.3) | copy-start | bytes 772
  23.2 5.4 %collective-permute-start.9 = (f32[144,128]{1,0:T(8,128)S(1)}, f32[144,128]{1,0:T(8,128)S(1)}, u32[]{:S(2)}, u32[]{:S(2)}) collective-permute-start(f32[144,128]{1,0:T(8,128)S(1)} %add_add_fusion.refs_0_), channel_id=1, source_target_pairs={{0,6},{1,7},{2,4},{3,5},{4,2},{5,3},{6,0},{7,1},{8,14},{9,15},{10,... | collective-permute-start | bytes 221192 | tf_op jit(solution)/shard_map/ppermute | solution.py:516
  24.0 5.1 %collective-permute-start.8 = (f32[144,128]{1,0:T(8,128)S(1)}, f32[144,128]{1,0:T(8,128)S(1)}, u32[]{:S(2)}, u32[]{:S(2)}) collective-permute-start(f32[144,128]{1,0:T(8,128)S(1)} %add_add_fusion.refs_0_), channel_id=1, source_target_pairs={{0,4},{1,5},{2,6},{3,7},{4,0},{5,1},{6,2},{7,3},{8,12},{9,13},{10,... | collective-permute-start | bytes 221192 | tf_op jit(solution)/shard_map/ppermute | solution.py:516
  25.5 4.4 %collective-permute-start.7 = (f32[144,128]{1,0:T(8,128)S(1)}, f32[144,128]{1,0:T(8,128)S(1)}, u32[]{:S(2)}, u32[]{:S(2)}) collective-permute-start(f32[144,128]{1,0:T(8,128)S(1)} %add_add_fusion.refs_0_), channel_id=1, source_target_pairs={{0,2},{1,3},{2,0},{3,1},{4,6},{5,7},{6,4},{7,5},{8,10},{9,11},{10,... | collective-permute-start | bytes 221192 | tf_op jit(solution)/shard_map/ppermute | solution.py:516
  26.8 3.1 %collective-permute-start.10 = (f32[144,128]{1,0:T(8,128)S(1)}, f32[144,128]{1,0:T(8,128)S(1)}, u32[]{:S(2)}, u32[]{:S(2)}) collective-permute-start(f32[144,128]{1,0:T(8,128)S(1)} %add_add_fusion.refs_0_), channel_id=1, source_target_pairs={{0,1},{1,0},{2,3},{3,2},{4,5},{5,4},{6,7},{7,6},{8,9},{9,8},{10,11... | collective-permute-start | bytes 221192 | tf_op jit(solution)/shard_map/ppermute | solution.py:516
  28.7 1.3 %collective-permute-start.13 = (f32[144,128]{1,0:T(8,128)S(1)}, f32[144,128]{1,0:T(8,128)S(1)}, u32[]{:S(2)}, u32[]{:S(2)}) collective-permute-start(f32[144,128]{1,0:T(8,128)S(1)} %collective-permute-done.9.refs_3_), channel_id=1, source_target_pairs={{0,1},{1,0},{2,3},{3,2},{4,5},{5,4},{6,7},{7,6},{8,9},{9,8},{10,11... | collective-permute-start | bytes 221192 | tf_op jit(solution)/shard_map/ppermute | solution.py:516
  29.2 1.3 %collective-permute-start.12 = (f32[144,128]{1,0:T(8,128)S(1)}, f32[144,128]{1,0:T(8,128)S(1)}, u32[]{:S(2)}, u32[]{:S(2)}) collective-permute-start(f32[144,128]{1,0:T(8,128)S(1)} %collective-permute-done.8.refs_2_), channel_id=1, source_target_pairs={{0,1},{1,0},{2,3},{3,2},{4,5},{5,4},{6,7},{7,6},{8,9},{9,8},{10,11... | collective-permute-start | bytes 221192 | tf_op jit(solution)/shard_map/ppermute | solution.py:516
  29.8 1.3 %collective-permute-start.11 = (f32[144,128]{1,0:T(8,128)S(1)}, f32[144,128]{1,0:T(8,128)S(1)}, u32[]{:S(2)}, u32[]{:S(2)}) collective-permute-start(f32[144,128]{1,0:T(8,128)S(1)} %collective-permute-done.7.refs_1_), channel_id=1, source_target_pairs={{0,1},{1,0},{2,3},{3,2},{4,5},{5,4},{6,7},{7,6},{8,9},{9,8},{10,11... | collective-permute-start | bytes 221192 | tf_op jit(solution)/shard_map/ppermute | solution.py:516

commit v4 on v3

--- a/solution.py
+++ b/solution.py
@@ -51,7 +51,7 @@
 
 
 def lane(x, c):
-    return jnp.broadcast_to(x[:, c : c + 1], (8, 128))
+    return jnp.take_along_axis(x, jnp.full((8, 128), c, jnp.int32), axis=1, mode="promise_in_bounds")
 
 
 def sub(x, i):

time: 48.8 us -> 48.8 us (level)
  no operation moved by 1% of the time
where the time goes in v4:
time: 48.8 us; the launch traced here: 48.6 us
  Pallas kernels  20.4 us (42%)
  waiting for transfers between devices  14.2 us (29%)
  starting transfers between devices  13 us (27%)
  between operations  0.86 us (2%)
    pallas_call x1, Pallas kernels, fit_call(): pl.pallas_call(body, out_shape=(jax.ShapeDtypeStruct((512, 512), f32), ja...  17.4 us
    ppermute x14, waiting for transfers between devices, swap(): return lax.ppermute(x, AXES, [(i, i ^ bit) for i in range(devices)])  14.2 us
    ppermute x14, starting transfers between devices, swap(): return lax.ppermute(x, AXES, [(i, i ^ bit) for i in range(devices)])  13 us
    pallas_call x1, Pallas kernels, gram_calls(): pl.pallas_call(first_kernel, out_shape=(half, jax.ShapeDtypeStruct(x.shap...  2.05 us
    pallas_call x1, Pallas kernels, gram_calls(): pl.pallas_call(second_kernel, out_shape=half, compiler_params=pltpu.Compi...  1 us
  transfers between devices with their start and end apart: 14, of which 11 were waited for; matrix products, arithmetic and copies ran while one was open for 0% of the time, Pallas kernels for 2%

profile of v4, /device:TPU:0, one launch (start us, length us, event | category | flops | bytes accessed | tf_op | source)
XLA Modules:
  0.0 48.6 jit_solution(11786562523781989013)
XLA Ops:
  0.6 2.0 %gram_other.1 = (f32[576,128]{1,0:T(8,128)S(1)}, f32[512,512]{1,0:T(8,128)S(1)}) custom-call(f32[512,512]{1,0:T(8,128)} %x_hbm.1), custom_call_target="tpu_custom_call" | custom-call | flops 503316480 | bytes 2097152 | tf_op jit(solution)/shard_map/gram_other/pallas_call | solution.py:478
  2.7 0.5 %collective-permute-start = (f32[576,128]{1,0:T(8,128)S(1)}, f32[576,128]{1,0:T(8,128)S(1)}, u32[]{:S(2)}, u32[]{:S(2)}) collective-permute-start(f32[576,128]{1,0:T(8,128)S(1)} %get-tuple-element.15), channel_id=1, source_target_pairs={{0,1},{1,0},{2,3},{3,2},{4,5},{5,4},{6,7},{7,6},{8,9},{9,8},{10,11... | collective-permute-start | bytes 884744 | tf_op jit(solution)/shard_map/ppermute | solution.py:516
  3.2 1.0 %gram_own.1.own_ref = f32[576,128]{1,0:T(8,128)S(1)} custom-call(f32[512,512]{1,0:T(8,128)S(1)} %get-tuple-element.14.x_ref.refs_8_), custom_call_target="tpu_custom_call" | custom-call | flops 503316480 | bytes 2097152 | tf_op jit(solution)/shard_map/gram_own/pallas_call | solution.py:488
  4.2 0.2 collective-permute-done.got_ref
  4.4 2.9 %collective-permute-start.1 = (f32[144,128]{1,0:T(8,128)S(1)}, f32[144,128]{1,0:T(8,128)S(1)}, u32[]{:S(2)}, u32[]{:S(2)}) collective-permute-start(f32[144,128]{1,0:T(8,128)S(1)} %get-tuple-element.17), channel_id=1, source_target_pairs={{0,2},{1,3},{2,0},{3,1},{4,6},{5,7},{6,4},{7,5},{8,10},{9,11},{10,... | collective-permute-start | bytes 221192 | tf_op jit(solution)/shard_map/ppermute | solution.py:516
  7.4 1.5 %collective-permute-start.2 = (f32[144,128]{1,0:T(8,128)S(1)}, f32[144,128]{1,0:T(8,128)S(1)}, u32[]{:S(2)}, u32[]{:S(2)}) collective-permute-start(f32[144,128]{1,0:T(8,128)S(1)} %get-tuple-element.18), channel_id=1, source_target_pairs={{0,4},{1,5},{2,6},{3,7},{4,0},{5,1},{6,2},{7,3},{8,12},{9,13},{10,... | collective-permute-start | bytes 221192 | tf_op jit(solution)/shard_map/ppermute | solution.py:516
  8.9 0.0 collective-permute-start.3
  8.9 1.0 %collective-permute-done.1 = f32[144,128]{1,0:T(8,128)S(1)} collective-permute-done((f32[144,128]{1,0:T(8,128)S(1)}, f32[144,128]{1,0:T(8,128)S(1)}, u32[]{:S(2)}, u32[]{:S(2)}) %collective-permute-start.1) | collective-permute-done | bytes 73760 | tf_op jit(solution)/shard_map/ppermute | solution.py:516
  9.9 1.8 %collective-permute-done.2 = f32[144,128]{1,0:T(8,128)S(1)} collective-permute-done((f32[144,128]{1,0:T(8,128)S(1)}, f32[144,128]{1,0:T(8,128)S(1)}, u32[]{:S(2)}, u32[]{:S(2)}) %collective-permute-start.2) | collective-permute-done | bytes 73760 | tf_op jit(solution)/shard_map/ppermute | solution.py:516
  11.7 2.4 %collective-permute-done.3 = f32[144,128]{1,0:T(8,128)S(1)} collective-permute-done((f32[144,128]{1,0:T(8,128)S(1)}, f32[144,128]{1,0:T(8,128)S(1)}, u32[]{:S(2)}, u32[]{:S(2)}) %collective-permute-start.3) | collective-permute-done | bytes 73760 | tf_op jit(solution)/shard_map/ppermute | solution.py:516
  14.2 3.7 %collective-permute-start.6 = (f32[144,128]{1,0:T(8,128)S(1)}, f32[144,128]{1,0:T(8,128)S(1)}, u32[]{:S(2)}, u32[]{:S(2)}) collective-permute-start(f32[144,128]{1,0:T(8,128)S(1)} %add_add_fusion.1), channel_id=1, source_target_pairs={{0,24},{1,25},{2,26},{3,27},{4,28},{5,29},{6,30},{7,31},{8,16},{9,... | collective-permute-start | bytes 221192 | tf_op jit(solution)/shard_map/ppermute | solution.py:516
  17.8 0.0 collective-permute-start.5
  17.8 0.8 %collective-permute-start.4 = (f32[144,128]{1,0:T(8,128)S(1)}, f32[144,128]{1,0:T(8,128)S(1)}, u32[]{:S(2)}, u32[]{:S(2)}) collective-permute-start(f32[144,128]{1,0:T(8,128)S(1)} %add_add_fusion.1), channel_id=1, source_target_pairs={{0,8},{1,9},{2,10},{3,11},{4,12},{5,13},{6,14},{7,15},{8,0},{9,1},... | collective-permute-start | bytes 221192 | tf_op jit(solution)/shard_map/ppermute | solution.py:516
  18.6 1.8 %collective-permute-done.6 = f32[144,128]{1,0:T(8,128)S(1)} collective-permute-done((f32[144,128]{1,0:T(8,128)S(1)}, f32[144,128]{1,0:T(8,128)S(1)}, u32[]{:S(2)}, u32[]{:S(2)}) %collective-permute-start.6) | collective-permute-done | bytes 73760 | tf_op jit(solution)/shard_map/ppermute | solution.py:516
  20.4 2.8 %collective-permute-done.5 = f32[144,128]{1,0:T(8,128)S(1)} collective-permute-done((f32[144,128]{1,0:T(8,128)S(1)}, f32[144,128]{1,0:T(8,128)S(1)}, u32[]{:S(2)}, u32[]{:S(2)}) %collective-permute-start.5) | collective-permute-done | bytes 73760 | tf_op jit(solution)/shard_map/ppermute | solution.py:516
  23.2 0.0 collective-permute-done.4
  23.2 0.0 copy-start
  23.2 0.8 %collective-permute-start.9 = (f32[144,128]{1,0:T(8,128)S(1)}, f32[144,128]{1,0:T(8,128)S(1)}, u32[]{:S(2)}, u32[]{:S(2)}) collective-permute-start(f32[144,128]{1,0:T(8,128)S(1)} %add_add_fusion.refs_0_), channel_id=1, source_target_pairs={{0,6},{1,7},{2,4},{3,5},{4,2},{5,3},{6,0},{7,1},{8,14},{9,15},{10,... | collective-permute-start | bytes 221192 | tf_op jit(solution)/shard_map/ppermute | solution.py:516
  24.0 1.5 %collective-permute-start.8 = (f32[144,128]{1,0:T(8,128)S(1)}, f32[144,128]{1,0:T(8,128)S(1)}, u32[]{:S(2)}, u32[]{:S(2)}) collective-permute-start(f32[144,128]{1,0:T(8,128)S(1)} %add_add_fusion.refs_0_), channel_id=1, source_target_pairs={{0,4},{1,5},{2,6},{3,7},{4,0},{5,1},{6,2},{7,3},{8,12},{9,13},{10,... | collective-permute-start | bytes 221192 | tf_op jit(solution)/shard_map/ppermute | solution.py:516
  25.5 1.3 %collective-permute-start.7 = (f32[144,128]{1,0:T(8,128)S(1)}, f32[144,128]{1,0:T(8,128)S(1)}, u32[]{:S(2)}, u32[]{:S(2)}) collective-permute-start(f32[144,128]{1,0:T(8,128)S(1)} %add_add_fusion.refs_0_), channel_id=1, source_target_pairs={{0,2},{1,3},{2,0},{3,1},{4,6},{5,7},{6,4},{7,5},{8,10},{9,11},{10,... | collective-permute-start | bytes 221192 | tf_op jit(solution)/shard_map/ppermute | solution.py:516
  26.8 0.0 collective-permute-start.10
  26.8 1.9 %collective-permute-done.9.refs_3_ = f32[144,128]{1,0:T(8,128)S(1)} collective-permute-done((f32[144,128]{1,0:T(8,128)S(1)}, f32[144,128]{1,0:T(8,128)S(1)}, u32[]{:S(2)}, u32[]{:S(2)}) %collective-permute-start.9) | collective-permute-done | bytes 73760 | tf_op jit(solution)/shard_map/ppermute | solution.py:516
  28.7 0.0 collective-permute-start.13
  28.7 0.5 %collective-permute-done.8.refs_2_ = f32[144,128]{1,0:T(8,128)S(1)} collective-permute-done((f32[144,128]{1,0:T(8,128)S(1)}, f32[144,128]{1,0:T(8,128)S(1)}, u32[]{:S(2)}, u32[]{:S(2)}) %collective-permute-start.8) | collective-permute-done | bytes 73760 | tf_op jit(solution)/shard_map/ppermute | solution.py:516
  29.2 0.0 collective-permute-start.12
  29.2 0.7 %collective-permute-done.7.refs_1_ = f32[144,128]{1,0:T(8,128)S(1)} collective-permute-done((f32[144,128]{1,0:T(8,128)S(1)}, f32[144,128]{1,0:T(8,128)S(1)}, u32[]{:S(2)}, u32[]{:S(2)}) %collective-permute-start.7) | collective-permute-done | bytes 73760 | tf_op jit(solution)/shard_map/ppermute | solution.py:516
  29.8 0.0 collective-permute-start.11
  29.8 0.0 copy-done
  29.8 0.1 copy.6.refs_9_
  29.9 0.0 collective-permute-done.10.refs_4_
  29.9 0.0 collective-permute-done.13.refs_7_
  30.0 0.5 collective-permute-done.12.refs_6_
  30.4 0.7 %collective-permute-done.11.refs_5_ = f32[144,128]{1,0:T(8,128)S(1)} collective-permute-done((f32[144,128]{1,0:T(8,128)S(1)}, f32[144,128]{1,0:T(8,128)S(1)}, u32[]{:S(2)}, u32[]{:S(2)}) %collective-permute-start.11) | collective-permute-done | bytes 73760 | tf_op jit(solution)/shard_map/ppermute | solution.py:516
  31.1 17.4 %factor_fit.1 = (f32[512,512]{1,0:T(8,128)}, f32[64,512]{1,0:T(8,128)}, f32[512,512]{1,0:T(8,128)}, f32[1,512]{1,0:T(1,128)}) custom-call(f32[144,128]{1,0:T(8,128)S(1)} %add_add_fusion.refs_0_, f32[144,128]{1,0:T(8,128)S(1)} %collective-permute-done.7.refs_1_, f32[144,128]{1,0:T(8,128)S(1)} %collective-permute-done.8.refs_2_, ...), custom_call_target="tpu_custom_call" | custom-call | tf_op jit(solution)/shard_map/factor_fit/pallas_call | solution.py:399
  (3 shorter events, 0.1 us)
Async XLA Ops:
  2.7 1.7 %collective-permute-start = (f32[576,128]{1,0:T(8,128)S(1)}, f32[576,128]{1,0:T(8,128)S(1)}, u32[]{:S(2)}, u32[]{:S(2)}) collective-permute-start(f32[576,128]{1,0:T(8,128)S(1)} %get-tuple-element.15), channel_id=1, source_target_pairs={{0,1},{1,0},{2,3},{3,2},{4,5},{5,4},{6,7},{7,6},{8,9},{9,8},{10,11... | collective-permute-start | bytes 884744 | tf_op jit(solution)/shard_map/ppermute | solution.py:516
  4.4 5.5 %collective-permute-start.1 = (f32[144,128]{1,0:T(8,128)S(1)}, f32[144,128]{1,0:T(8,128)S(1)}, u32[]{:S(2)}, u32[]{:S(2)}) collective-permute-start(f32[144,128]{1,0:T(8,128)S(1)} %get-tuple-element.17), channel_id=1, source_target_pairs={{0,2},{1,3},{2,0},{3,1},{4,6},{5,7},{6,4},{7,5},{8,10},{9,11},{10,... | collective-permute-start | bytes 221192 | tf_op jit(solution)/shard_map/ppermute | solution.py:516
  7.4 4.4 %collective-permute-start.2 = (f32[144,128]{1,0:T(8,128)S(1)}, f32[144,128]{1,0:T(8,128)S(1)}, u32[]{:S(2)}, u32[]{:S(2)}) collective-permute-start(f32[144,128]{1,0:T(8,128)S(1)} %get-tuple-element.18), channel_id=1, source_target_pairs={{0,4},{1,5},{2,6},{3,7},{4,0},{5,1},{6,2},{7,3},{8,12},{9,13},{10,... | collective-permute-start | bytes 221192 | tf_op jit(solution)/shard_map/ppermute | solution.py:516
  8.9 5.3 %collective-permute-start.3 = (f32[144,128]{1,0:T(8,128)S(1)}, f32[144,128]{1,0:T(8,128)S(1)}, u32[]{:S(2)}, u32[]{:S(2)}) collective-permute-start(f32[144,128]{1,0:T(8,128)S(1)} %get-tuple-element.19), channel_id=1, source_target_pairs={{0,6},{1,7},{2,4},{3,5},{4,2},{5,3},{6,0},{7,1},{8,14},{9,15},{10,... | collective-permute-start | bytes 221192 | tf_op jit(solution)/shard_map/ppermute | solution.py:516
  14.2 6.2 %collective-permute-start.6 = (f32[144,128]{1,0:T(8,128)S(1)}, f32[144,128]{1,0:T(8,128)S(1)}, u32[]{:S(2)}, u32[]{:S(2)}) collective-permute-start(f32[144,128]{1,0:T(8,128)S(1)} %add_add_fusion.1), channel_id=1, source_target_pairs={{0,24},{1,25},{2,26},{3,27},{4,28},{5,29},{6,30},{7,31},{8,16},{9,... | collective-permute-start | bytes 221192 | tf_op jit(solution)/shard_map/ppermute | solution.py:516
  17.8 5.4 %collective-permute-start.5 = (f32[144,128]{1,0:T(8,128)S(1)}, f32[144,128]{1,0:T(8,128)S(1)}, u32[]{:S(2)}, u32[]{:S(2)}) collective-permute-start(f32[144,128]{1,0:T(8,128)S(1)} %add_add_fusion.1), channel_id=1, source_target_pairs={{0,16},{1,17},{2,18},{3,19},{4,20},{5,21},{6,22},{7,23},{8,24},{9,... | collective-permute-start | bytes 221192 | tf_op jit(solution)/shard_map/ppermute | solution.py:516
  17.8 5.4 %collective-permute-start.4 = (f32[144,128]{1,0:T(8,128)S(1)}, f32[144,128]{1,0:T(8,128)S(1)}, u32[]{:S(2)}, u32[]{:S(2)}) collective-permute-start(f32[144,128]{1,0:T(8,128)S(1)} %add_add_fusion.1), channel_id=1, source_target_pairs={{0,8},{1,9},{2,10},{3,11},{4,12},{5,13},{6,14},{7,15},{8,0},{9,1},... | collective-permute-start | bytes 221192 | tf_op jit(solution)/shard_map/ppermute | solution.py:516
  23.2 6.6 %copy-start = (s32[64]{0:T(128)S(1)}, s32[64]{0:T(128)}, u32[]{:S(2)}) copy-start(s32[64]{0:T(128)} %param.3) | copy-start | bytes 772
  23.2 5.4 %collective-permute-start.9 = (f32[144,128]{1,0:T(8,128)S(1)}, f32[144,128]{1,0:T(8,128)S(1)}, u32[]{:S(2)}, u32[]{:S(2)}) collective-permute-start(f32[144,128]{1,0:T(8,128)S(1)} %add_add_fusion.refs_0_), channel_id=1, source_target_pairs={{0,6},{1,7},{2,4},{3,5},{4,2},{5,3},{6,0},{7,1},{8,14},{9,15},{10,... | collective-permute-start | bytes 221192 | tf_op jit(solution)/shard_map/ppermute | solution.py:516
  24.0 5.1 %collective-permute-start.8 = (f32[144,128]{1,0:T(8,128)S(1)}, f32[144,128]{1,0:T(8,128)S(1)}, u32[]{:S(2)}, u32[]{:S(2)}) collective-permute-start(f32[144,128]{1,0:T(8,128)S(1)} %add_add_fusion.refs_0_), channel_id=1, source_target_pairs={{0,4},{1,5},{2,6},{3,7},{4,0},{5,1},{6,2},{7,3},{8,12},{9,13},{10,... | collective-permute-start | bytes 221192 | tf_op jit(solution)/shard_map/ppermute | solution.py:516
  25.5 4.4 %collective-permute-start.7 = (f32[144,128]{1,0:T(8,128)S(1)}, f32[144,128]{1,0:T(8,128)S(1)}, u32[]{:S(2)}, u32[]{:S(2)}) collective-permute-start(f32[144,128]{1,0:T(8,128)S(1)} %add_add_fusion.refs_0_), channel_id=1, source_target_pairs={{0,2},{1,3},{2,0},{3,1},{4,6},{5,7},{6,4},{7,5},{8,10},{9,11},{10,... | collective-permute-start | bytes 221192 | tf_op jit(solution)/shard_map/ppermute | solution.py:516
  26.8 3.1 %collective-permute-start.10 = (f32[144,128]{1,0:T(8,128)S(1)}, f32[144,128]{1,0:T(8,128)S(1)}, u32[]{:S(2)}, u32[]{:S(2)}) collective-permute-start(f32[144,128]{1,0:T(8,128)S(1)} %add_add_fusion.refs_0_), channel_id=1, source_target_pairs={{0,1},{1,0},{2,3},{3,2},{4,5},{5,4},{6,7},{7,6},{8,9},{9,8},{10,11... | collective-permute-start | bytes 221192 | tf_op jit(solution)/shard_map/ppermute | solution.py:516
  28.7 1.3 %collective-permute-start.13 = (f32[144,128]{1,0:T(8,128)S(1)}, f32[144,128]{1,0:T(8,128)S(1)}, u32[]{:S(2)}, u32[]{:S(2)}) collective-permute-start(f32[144,128]{1,0:T(8,128)S(1)} %collective-permute-done.9.refs_3_), channel_id=1, source_target_pairs={{0,1},{1,0},{2,3},{3,2},{4,5},{5,4},{6,7},{7,6},{8,9},{9,8},{10,11... | collective-permute-start | bytes 221192 | tf_op jit(solution)/shard_map/ppermute | solution.py:516
  29.2 1.3 %collective-permute-start.12 = (f32[144,128]{1,0:T(8,128)S(1)}, f32[144,128]{1,0:T(8,128)S(1)}, u32[]{:S(2)}, u32[]{:S(2)}) collective-permute-start(f32[144,128]{1,0:T(8,128)S(1)} %collective-permute-done.8.refs_2_), channel_id=1, source_target_pairs={{0,1},{1,0},{2,3},{3,2},{4,5},{5,4},{6,7},{7,6},{8,9},{9,8},{10,11... | collective-permute-start | bytes 221192 | tf_op jit(solution)/shard_map/ppermute | solution.py:516
  29.8 1.3 %collective-permute-start.11 = (f32[144,128]{1,0:T(8,128)S(1)}, f32[144,128]{1,0:T(8,128)S(1)}, u32[]{:S(2)}, u32[]{:S(2)}) collective-permute-start(f32[144,128]{1,0:T(8,128)S(1)} %collective-permute-done.7.refs_1_), channel_id=1, source_target_pairs={{0,1},{1,0},{2,3},{3,2},{4,5},{5,4},{6,7},{7,6},{8,9},{9,8},{10,11... | collective-permute-start | bytes 221192 | tf_op jit(solution)/shard_map/ppermute | solution.py:516

commit v5 on v4

--- a/solution.py
+++ b/solution.py
@@ -429,12 +429,13 @@
     return lax.axis_index("wide") * lax.axis_size("narrow") + lax.axis_index("narrow")
 
 
-def gram_half(x, half, out_ref):
+def gram_half(x, half, out_ref, add=False):
     n = 0
 
     def put(unit):
         nonlocal n
-        out_ref[64 * n : 64 * n + 64, :] = unit
+        at = slice(64 * n, 64 * n + 64)
+        out_ref[at, :] = out_ref[at, :] + unit if add else unit
         n += 1
 
     corners = []
@@ -458,11 +459,15 @@
         at = pl.ds(rows * c, rows)
         copies.append(pltpu.make_async_copy(x_hbm.at[at, :], x_ref.at[at, :], sem.at[c]))
         copies[-1].start()
-    for c in copies:
-        c.wait()
     bit = lax.rem(my_index(), 2)
-    for half in (0, 1):
-        pl.when(bit != half)(lambda half=half: gram_half(x_ref[...], half, out_ref))
+    for part in (0, 1):
+        for c in copies[2 * part : 2 * part + 2]:
+            c.wait()
+        at = slice(2 * rows * part, 2 * rows * part + 2 * rows)
+        for half in (0, 1):
+            pl.when(bit != half)(
+                lambda half=half, at=at, part=part: gram_half(x_ref[at, :], half, out_ref, add=part > 0)
+            )
 
 
 def second_kernel(x_ref, out_ref):

time: 48.8 us -> 48.8 us (level)
  no operation moved by 1% of the time
where the time goes in v5:
time: 48.8 us; the launch traced here: 48.7 us
  Pallas kernels  20.5 us (42%)
  waiting for transfers between devices  14.2 us (29%)
  starting transfers between devices  13 us (27%)
  between operations  0.86 us (2%)
    pallas_call x1, Pallas kernels, fit_call(): pl.pallas_call(body, out_shape=(jax.ShapeDtypeStruct((512, 512), f32), ja...  17.4 us
    ppermute x14, waiting for transfers between devices, swap(): return lax.ppermute(x, AXES, [(i, i ^ bit) for i in range(devices)])  14.2 us
    ppermute x14, starting transfers between devices, swap(): return lax.ppermute(x, AXES, [(i, i ^ bit) for i in range(devices)])  13 us
    pallas_call x1, Pallas kernels, gram_calls(): pl.pallas_call(first_kernel, out_shape=(half, jax.ShapeDtypeStruct(x.shap...  2.1 us
    pallas_call x1, Pallas kernels, gram_calls(): pl.pallas_call(second_kernel, out_shape=half, compiler_params=pltpu.Compi...  1 us
  transfers between devices with their start and end apart: 14, of which 11 were waited for; matrix products, arithmetic and copies ran while one was open for 0% of the time, Pallas kernels for 2%

profile of v5, /device:TPU:0, one launch (start us, length us, event | category | flops | bytes accessed | tf_op | source)
XLA Modules:
  0.0 48.7 jit_solution(13043998456350866082)
XLA Ops:
  0.6 2.1 %gram_other.1 = (f32[576,128]{1,0:T(8,128)S(1)}, f32[512,512]{1,0:T(8,128)S(1)}) custom-call(f32[512,512]{1,0:T(8,128)} %x_hbm.1), custom_call_target="tpu_custom_call" | custom-call | flops 503316480 | bytes 2097152 | tf_op jit(solution)/shard_map/gram_other/pallas_call | solution.py:483
  2.7 0.5 %collective-permute-start = (f32[576,128]{1,0:T(8,128)S(1)}, f32[576,128]{1,0:T(8,128)S(1)}, u32[]{:S(2)}, u32[]{:S(2)}) collective-permute-start(f32[576,128]{1,0:T(8,128)S(1)} %get-tuple-element.15), channel_id=1, source_target_pairs={{0,1},{1,0},{2,3},{3,2},{4,5},{5,4},{6,7},{7,6},{8,9},{9,8},{10,11... | collective-permute-start | bytes 884744 | tf_op jit(solution)/shard_map/ppermute | solution.py:521
  3.3 1.0 %gram_own.1.own_ref = f32[576,128]{1,0:T(8,128)S(1)} custom-call(f32[512,512]{1,0:T(8,128)S(1)} %get-tuple-element.14.x_ref.refs_8_), custom_call_target="tpu_custom_call" | custom-call | flops 503316480 | bytes 2097152 | tf_op jit(solution)/shard_map/gram_own/pallas_call | solution.py:493
  4.3 0.2 collective-permute-done.got_ref
  4.5 2.9 %collective-permute-start.1 = (f32[144,128]{1,0:T(8,128)S(1)}, f32[144,128]{1,0:T(8,128)S(1)}, u32[]{:S(2)}, u32[]{:S(2)}) collective-permute-start(f32[144,128]{1,0:T(8,128)S(1)} %get-tuple-element.17), channel_id=1, source_target_pairs={{0,2},{1,3},{2,0},{3,1},{4,6},{5,7},{6,4},{7,5},{8,10},{9,11},{10,... | collective-permute-start | bytes 221192 | tf_op jit(solution)/shard_map/ppermute | solution.py:521
  7.4 1.5 %collective-permute-start.2 = (f32[144,128]{1,0:T(8,128)S(1)}, f32[144,128]{1,0:T(8,128)S(1)}, u32[]{:S(2)}, u32[]{:S(2)}) collective-permute-start(f32[144,128]{1,0:T(8,128)S(1)} %get-tuple-element.18), channel_id=1, source_target_pairs={{0,4},{1,5},{2,6},{3,7},{4,0},{5,1},{6,2},{7,3},{8,12},{9,13},{10,... | collective-permute-start | bytes 221192 | tf_op jit(solution)/shard_map/ppermute | solution.py:521
  8.9 0.0 collective-permute-start.3
  9.0 1.0 %collective-permute-done.1 = f32[144,128]{1,0:T(8,128)S(1)} collective-permute-done((f32[144,128]{1,0:T(8,128)S(1)}, f32[144,128]{1,0:T(8,128)S(1)}, u32[]{:S(2)}, u32[]{:S(2)}) %collective-permute-start.1) | collective-permute-done | bytes 73760 | tf_op jit(solution)/shard_map/ppermute | solution.py:521
  10.0 1.8 %collective-permute-done.2 = f32[144,128]{1,0:T(8,128)S(1)} collective-permute-done((f32[144,128]{1,0:T(8,128)S(1)}, f32[144,128]{1,0:T(8,128)S(1)}, u32[]{:S(2)}, u32[]{:S(2)}) %collective-permute-start.2) | collective-permute-done | bytes 73760 | tf_op jit(solution)/shard_map/ppermute | solution.py:521
  11.8 2.4 %collective-permute-done.3 = f32[144,128]{1,0:T(8,128)S(1)} collective-permute-done((f32[144,128]{1,0:T(8,128)S(1)}, f32[144,128]{1,0:T(8,128)S(1)}, u32[]{:S(2)}, u32[]{:S(2)}) %collective-permute-start.3) | collective-permute-done | bytes 73760 | tf_op jit(solution)/shard_map/ppermute | solution.py:521
  14.2 3.7 %collective-permute-start.6 = (f32[144,128]{1,0:T(8,128)S(1)}, f32[144,128]{1,0:T(8,128)S(1)}, u32[]{:S(2)}, u32[]{:S(2)}) collective-permute-start(f32[144,128]{1,0:T(8,128)S(1)} %add_add_fusion.1), channel_id=1, source_target_pairs={{0,24},{1,25},{2,26},{3,27},{4,28},{5,29},{6,30},{7,31},{8,16},{9,... | collective-permute-start | bytes 221192 | tf_op jit(solution)/shard_map/ppermute | solution.py:521
  17.9 0.0 collective-permute-start.5
  17.9 0.8 %collective-permute-start.4 = (f32[144,128]{1,0:T(8,128)S(1)}, f32[144,128]{1,0:T(8,128)S(1)}, u32[]{:S(2)}, u32[]{:S(2)}) collective-permute-start(f32[144,128]{1,0:T(8,128)S(1)} %add_add_fusion.1), channel_id=1, source_target_pairs={{0,8},{1,9},{2,10},{3,11},{4,12},{5,13},{6,14},{7,15},{8,0},{9,1},... | collective-permute-start | bytes 221192 | tf_op jit(solution)/shard_map/ppermute | solution.py:521
  18.7 1.8 %collective-permute-done.6 = f32[144,128]{1,0:T(8,128)S(1)} collective-permute-done((f32[144,128]{1,0:T(8,128)S(1)}, f32[144,128]{1,0:T(8,128)S(1)}, u32[]{:S(2)}, u32[]{:S(2)}) %collective-permute-start.6) | collective-permute-done | bytes 73760 | tf_op jit(solution)/shard_map/ppermute | solution.py:521
  20.4 2.8 %collective-permute-done.5 = f32[144,128]{1,0:T(8,128)S(1)} collective-permute-done((f32[144,128]{1,0:T(8,128)S(1)}, f32[144,128]{1,0:T(8,128)S(1)}, u32[]{:S(2)}, u32[]{:S(2)}) %collective-permute-start.5) | collective-permute-done | bytes 73760 | tf_op jit(solution)/shard_map/ppermute | solution.py:521
  23.3 0.0 collective-permute-done.4
  23.3 0.0 copy-start
  23.3 0.8 %collective-permute-start.9 = (f32[144,128]{1,0:T(8,128)S(1)}, f32[144,128]{1,0:T(8,128)S(1)}, u32[]{:S(2)}, u32[]{:S(2)}) collective-permute-start(f32[144,128]{1,0:T(8,128)S(1)} %add_add_fusion.refs_0_), channel_id=1, source_target_pairs={{0,6},{1,7},{2,4},{3,5},{4,2},{5,3},{6,0},{7,1},{8,14},{9,15},{10,... | collective-permute-start | bytes 221192 | tf_op jit(solution)/shard_map/ppermute | solution.py:521
  24.1 1.5 %collective-permute-start.8 = (f32[144,128]{1,0:T(8,128)S(1)}, f32[144,128]{1,0:T(8,128)S(1)}, u32[]{:S(2)}, u32[]{:S(2)}) collective-permute-start(f32[144,128]{1,0:T(8,128)S(1)} %add_add_fusion.refs_0_), channel_id=1, source_target_pairs={{0,4},{1,5},{2,6},{3,7},{4,0},{5,1},{6,2},{7,3},{8,12},{9,13},{10,... | collective-permute-start | bytes 221192 | tf_op jit(solution)/shard_map/ppermute | solution.py:521
  25.5 1.3 %collective-permute-start.7 = (f32[144,128]{1,0:T(8,128)S(1)}, f32[144,128]{1,0:T(8,128)S(1)}, u32[]{:S(2)}, u32[]{:S(2)}) collective-permute-start(f32[144,128]{1,0:T(8,128)S(1)} %add_add_fusion.refs_0_), channel_id=1, source_target_pairs={{0,2},{1,3},{2,0},{3,1},{4,6},{5,7},{6,4},{7,5},{8,10},{9,11},{10,... | collective-permute-start | bytes 221192 | tf_op jit(solution)/shard_map/ppermute | solution.py:521
  26.9 0.0 collective-permute-start.10
  26.9 1.9 %collective-permute-done.9.refs_3_ = f32[144,128]{1,0:T(8,128)S(1)} collective-permute-done((f32[144,128]{1,0:T(8,128)S(1)}, f32[144,128]{1,0:T(8,128)S(1)}, u32[]{:S(2)}, u32[]{:S(2)}) %collective-permute-start.9) | collective-permute-done | bytes 73760 | tf_op jit(solution)/shard_map/ppermute | solution.py:521
  28.7 0.0 collective-permute-start.13
  28.7 0.5 %collective-permute-done.8.refs_2_ = f32[144,128]{1,0:T(8,128)S(1)} collective-permute-done((f32[144,128]{1,0:T(8,128)S(1)}, f32[144,128]{1,0:T(8,128)S(1)}, u32[]{:S(2)}, u32[]{:S(2)}) %collective-permute-start.8) | collective-permute-done | bytes 73760 | tf_op jit(solution)/shard_map/ppermute | solution.py:521
  29.2 0.0 collective-permute-start.12
  29.2 0.6 %collective-permute-done.7.refs_1_ = f32[144,128]{1,0:T(8,128)S(1)} collective-permute-done((f32[144,128]{1,0:T(8,128)S(1)}, f32[144,128]{1,0:T(8,128)S(1)}, u32[]{:S(2)}, u32[]{:S(2)}) %collective-permute-start.7) | collective-permute-done | bytes 73760 | tf_op jit(solution)/shard_map/ppermute | solution.py:521
  29.9 0.0 collective-permute-start.11
  29.9 0.0 copy-done
  29.9 0.1 copy.6.refs_9_
  30.0 0.0 collective-permute-done.10.refs_4_
  30.0 0.0 collective-permute-done.13.refs_7_
  30.0 0.5 collective-permute-done.12.refs_6_
  30.5 0.7 %collective-permute-done.11.refs_5_ = f32[144,128]{1,0:T(8,128)S(1)} collective-permute-done((f32[144,128]{1,0:T(8,128)S(1)}, f32[144,128]{1,0:T(8,128)S(1)}, u32[]{:S(2)}, u32[]{:S(2)}) %collective-permute-start.11) | collective-permute-done | bytes 73760 | tf_op jit(solution)/shard_map/ppermute | solution.py:521
  31.2 17.4 %factor_fit.1 = (f32[512,512]{1,0:T(8,128)}, f32[64,512]{1,0:T(8,128)}, f32[512,512]{1,0:T(8,128)}, f32[1,512]{1,0:T(1,128)}) custom-call(f32[144,128]{1,0:T(8,128)S(1)} %add_add_fusion.refs_0_, f32[144,128]{1,0:T(8,128)S(1)} %collective-permute-done.7.refs_1_, f32[144,128]{1,0:T(8,128)S(1)} %collective-permute-done.8.refs_2_, ...), custom_call_target="tpu_custom_call" | custom-call | tf_op jit(solution)/shard_map/factor_fit/pallas_call | solution.py:399
  (3 shorter events, 0.1 us)
Async XLA Ops:
  2.7 1.7 %collective-permute-start = (f32[576,128]{1,0:T(8,128)S(1)}, f32[576,128]{1,0:T(8,128)S(1)}, u32[]{:S(2)}, u32[]{:S(2)}) collective-permute-start(f32[576,128]{1,0:T(8,128)S(1)} %get-tuple-element.15), channel_id=1, source_target_pairs={{0,1},{1,0},{2,3},{3,2},{4,5},{5,4},{6,7},{7,6},{8,9},{9,8},{10,11... | collective-permute-start | bytes 884744 | tf_op jit(solution)/shard_map/ppermute | solution.py:521
  4.5 5.5 %collective-permute-start.1 = (f32[144,128]{1,0:T(8,128)S(1)}, f32[144,128]{1,0:T(8,128)S(1)}, u32[]{:S(2)}, u32[]{:S(2)}) collective-permute-start(f32[144,128]{1,0:T(8,128)S(1)} %get-tuple-element.17), channel_id=1, source_target_pairs={{0,2},{1,3},{2,0},{3,1},{4,6},{5,7},{6,4},{7,5},{8,10},{9,11},{10,... | collective-permute-start | bytes 221192 | tf_op jit(solution)/shard_map/ppermute | solution.py:521
  7.4 4.4 %collective-permute-start.2 = (f32[144,128]{1,0:T(8,128)S(1)}, f32[144,128]{1,0:T(8,128)S(1)}, u32[]{:S(2)}, u32[]{:S(2)}) collective-permute-start(f32[144,128]{1,0:T(8,128)S(1)} %get-tuple-element.18), channel_id=1, source_target_pairs={{0,4},{1,5},{2,6},{3,7},{4,0},{5,1},{6,2},{7,3},{8,12},{9,13},{10,... | collective-permute-start | bytes 221192 | tf_op jit(solution)/shard_map/ppermute | solution.py:521
  8.9 5.3 %collective-permute-start.3 = (f32[144,128]{1,0:T(8,128)S(1)}, f32[144,128]{1,0:T(8,128)S(1)}, u32[]{:S(2)}, u32[]{:S(2)}) collective-permute-start(f32[144,128]{1,0:T(8,128)S(1)} %get-tuple-element.19), channel_id=1, source_target_pairs={{0,6},{1,7},{2,4},{3,5},{4,2},{5,3},{6,0},{7,1},{8,14},{9,15},{10,... | collective-permute-start | bytes 221192 | tf_op jit(solution)/shard_map/ppermute | solution.py:521
  14.2 6.2 %collective-permute-start.6 = (f32[144,128]{1,0:T(8,128)S(1)}, f32[144,128]{1,0:T(8,128)S(1)}, u32[]{:S(2)}, u32[]{:S(2)}) collective-permute-start(f32[144,128]{1,0:T(8,128)S(1)} %add_add_fusion.1), channel_id=1, source_target_pairs={{0,24},{1,25},{2,26},{3,27},{4,28},{5,29},{6,30},{7,31},{8,16},{9,... | collective-permute-start | bytes 221192 | tf_op jit(solution)/shard_map/ppermute | solution.py:521
  17.9 5.4 %collective-permute-start.5 = (f32[144,128]{1,0:T(8,128)S(1)}, f32[144,128]{1,0:T(8,128)S(1)}, u32[]{:S(2)}, u32[]{:S(2)}) collective-permute-start(f32[144,128]{1,0:T(8,128)S(1)} %add_add_fusion.1), channel_id=1, source_target_pairs={{0,16},{1,17},{2,18},{3,19},{4,20},{5,21},{6,22},{7,23},{8,24},{9,... | collective-permute-start | bytes 221192 | tf_op jit(solution)/shard_map/ppermute | solution.py:521
  17.9 5.4 %collective-permute-start.4 = (f32[144,128]{1,0:T(8,128)S(1)}, f32[144,128]{1,0:T(8,128)S(1)}, u32[]{:S(2)}, u32[]{:S(2)}) collective-permute-start(f32[144,128]{1,0:T(8,128)S(1)} %add_add_fusion.1), channel_id=1, source_target_pairs={{0,8},{1,9},{2,10},{3,11},{4,12},{5,13},{6,14},{7,15},{8,0},{9,1},... | collective-permute-start | bytes 221192 | tf_op jit(solution)/shard_map/ppermute | solution.py:521
  23.3 6.6 %copy-start = (s32[64]{0:T(128)S(1)}, s32[64]{0:T(128)}, u32[]{:S(2)}) copy-start(s32[64]{0:T(128)} %param.3) | copy-start | bytes 772
  23.3 5.4 %collective-permute-start.9 = (f32[144,128]{1,0:T(8,128)S(1)}, f32[144,128]{1,0:T(8,128)S(1)}, u32[]{:S(2)}, u32[]{:S(2)}) collective-permute-start(f32[144,128]{1,0:T(8,128)S(1)} %add_add_fusion.refs_0_), channel_id=1, source_target_pairs={{0,6},{1,7},{2,4},{3,5},{4,2},{5,3},{6,0},{7,1},{8,14},{9,15},{10,... | collective-permute-start | bytes 221192 | tf_op jit(solution)/shard_map/ppermute | solution.py:521
  24.1 5.1 %collective-permute-start.8 = (f32[144,128]{1,0:T(8,128)S(1)}, f32[144,128]{1,0:T(8,128)S(1)}, u32[]{:S(2)}, u32[]{:S(2)}) collective-permute-start(f32[144,128]{1,0:T(8,128)S(1)} %add_add_fusion.refs_0_), channel_id=1, source_target_pairs={{0,4},{1,5},{2,6},{3,7},{4,0},{5,1},{6,2},{7,3},{8,12},{9,13},{10,... | collective-permute-start | bytes 221192 | tf_op jit(solution)/shard_map/ppermute | solution.py:521
  25.5 4.4 %collective-permute-start.7 = (f32[144,128]{1,0:T(8,128)S(1)}, f32[144,128]{1,0:T(8,128)S(1)}, u32[]{:S(2)}, u32[]{:S(2)}) collective-permute-start(f32[144,128]{1,0:T(8,128)S(1)} %add_add_fusion.refs_0_), channel_id=1, source_target_pairs={{0,2},{1,3},{2,0},{3,1},{4,6},{5,7},{6,4},{7,5},{8,10},{9,11},{10,... | collective-permute-start | bytes 221192 | tf_op jit(solution)/shard_map/ppermute | solution.py:521
  26.9 3.1 %collective-permute-start.10 = (f32[144,128]{1,0:T(8,128)S(1)}, f32[144,128]{1,0:T(8,128)S(1)}, u32[]{:S(2)}, u32[]{:S(2)}) collective-permute-start(f32[144,128]{1,0:T(8,128)S(1)} %add_add_fusion.refs_0_), channel_id=1, source_target_pairs={{0,1},{1,0},{2,3},{3,2},{4,5},{5,4},{6,7},{7,6},{8,9},{9,8},{10,11... | collective-permute-start | bytes 221192 | tf_op jit(solution)/shard_map/ppermute | solution.py:521
  28.7 1.3 %collective-permute-start.13 = (f32[144,128]{1,0:T(8,128)S(1)}, f32[144,128]{1,0:T(8,128)S(1)}, u32[]{:S(2)}, u32[]{:S(2)}) collective-permute-start(f32[144,128]{1,0:T(8,128)S(1)} %collective-permute-done.9.refs_3_), channel_id=1, source_target_pairs={{0,1},{1,0},{2,3},{3,2},{4,5},{5,4},{6,7},{7,6},{8,9},{9,8},{10,11... | collective-permute-start | bytes 221192 | tf_op jit(solution)/shard_map/ppermute | solution.py:521
  29.2 1.3 %collective-permute-start.12 = (f32[144,128]{1,0:T(8,128)S(1)}, f32[144,128]{1,0:T(8,128)S(1)}, u32[]{:S(2)}, u32[]{:S(2)}) collective-permute-start(f32[144,128]{1,0:T(8,128)S(1)} %collective-permute-done.8.refs_2_), channel_id=1, source_target_pairs={{0,1},{1,0},{2,3},{3,2},{4,5},{5,4},{6,7},{7,6},{8,9},{9,8},{10,11... | collective-permute-start | bytes 221192 | tf_op jit(solution)/shard_map/ppermute | solution.py:521
  29.9 1.3 %collective-permute-start.11 = (f32[144,128]{1,0:T(8,128)S(1)}, f32[144,128]{1,0:T(8,128)S(1)}, u32[]{:S(2)}, u32[]{:S(2)}) collective-permute-start(f32[144,128]{1,0:T(8,128)S(1)} %collective-permute-done.7.refs_1_), channel_id=1, source_target_pairs={{0,1},{1,0},{2,3},{3,2},{4,5},{5,4},{6,7},{7,6},{8,9},{9,8},{10,11... | collective-permute-start | bytes 221192 | tf_op jit(solution)/shard_map/ppermute | solution.py:521
